TPU v7x, 32 devices: a whole 2x2x4 slice. The times are simulated.
32 devices in a mesh: clip: 2 (over y), row: 16 (over z, x, core).
Axes of the slice: x: 2, y: 2, z: 4, core: 2. Of those that a mesh axis runs over, the one named last changes fastest.
Arguments:
- frames: bfloat16 [3, 48, 512], P(None, None, ('clip', 'row')), parts along dimension 2, may hold values from -1 to 1
- frame_owner: int32 [32], P('clip'), parts along dimension 0, may hold values from 0 to 15, each once
- picks: int32 [16], P('clip'), parts along dimension 0, may hold values from 0 to 15
- patch_weight: bfloat16 [768, 1024], replicated, may hold values from -0.21875 to 0.21875
- patch_bias: float32 [1024], replicated, may hold values from -6 to 6
- norm_gain: float32 [1024], replicated, may hold values from 0.1 to 1.9
- head_weight: bfloat16 [1024, 1024], replicated, may hold values from -0.1875 to 0.1875
- head_bias: float32 [1024], replicated, may hold values from -6 to 6
- head_out: float32 [1024], replicated, may hold values from -6 to 6
- hidden_state: bfloat16 [96, 16, 16, 128], P(('clip', 'row')), parts along dimension 0
- group_gain: float32 [128], replicated, may hold values from 0.1 to 1.9
- group_shift: float32 [128], replicated, may hold values from -6 to 6
- out_weight: bfloat16 [3, 3, 3, 3, 128], replicated, may hold values from -0.625 to 0.625
- inner_weight: bfloat16 [3, 3, 3, 128, 128], replicated, may hold values from -0.109375 to 0.109375
Outputs:
- inner_grad: bfloat16 [96, 16, 16, 128], P(('clip', 'row')), parts along dimension 0
There are 2 independent parts, one for each index of `clip`. A program takes and returns all parts, laid end to end along the dimension named above; an argument that names none is the same for every part. Nothing has to cross between parts.
Inputs may be any that keep to these rules, and one draw needn't show every extreme that they name: `frame_owner`: each of the 16 frames appears once.
All inputs are finite; a program needn't handle non-finite values.
Results may differ from a plain program's by a relative error of at most 0.0051.
The roundings to bfloat16 on the way count: a program that leaves them out, or rounds other values in their place, can miss the bound.
Values may be sent and summed in bfloat16 or wider, within the bound.
A program may use at most 192 MiB of HBM per device.

v0:
```python
import functools

import jax
import jax.numpy as jnp
from jax import lax
from jax.experimental import pallas as pl
from jax.experimental.pallas import tpu as pltpu
from jax.sharding import PartitionSpec as P

PATCH = 16
GROUPS = 32
FRAMES = 16


eps_norm = 1e-06
MESH = pl.DeviceIdType.MESH


def extended(block, sides, width):
    for axis, dim in sides:
        count = lax.axis_size(axis)
        forward = [(i, i + 1) for i in range(count - 1)]
        backward = [(target, source) for source, target in forward]
        low = lax.ppermute(
            lax.slice_in_dim(block, block.shape[dim] - width, None, axis=dim), axis, forward
        )
        high = lax.ppermute(lax.slice_in_dim(block, 0, width, axis=dim), axis, backward)
        block = jnp.concatenate([low, block, high], axis=dim)
    return block


def silu_slope(values):
    sigmoid = jax.nn.sigmoid(values)
    return sigmoid * (1.0 + values * (1.0 - sigmoid))


def to_tokens(pixels):
    channels, height, columns = pixels.shape
    shaped = pixels.reshape(channels, height // PATCH, PATCH, columns // PATCH, PATCH)
    return shaped.transpose(1, 3, 0, 2, 4).reshape(
        height // PATCH * (columns // PATCH), channels * PATCH * PATCH
    )


def from_tokens(token_grads, height, columns):
    shaped = token_grads.reshape(height // PATCH, columns // PATCH, 3, PATCH, PATCH)
    return shaped.transpose(2, 0, 3, 1, 4).reshape(3, height, columns)


def pixel_back(padded, out_weight, amount):
    frame_count = padded.shape[2]
    columns = padded.shape[3]
    widened = jnp.pad(padded, ((0, 0), (0, 0), (0, 2), (1, 1)))
    windows = []
    for time_tap in range(3):
        for row_tap in range(3):
            for col_tap in range(3):
                windows.append(
                    widened[
                        :,
                        2 - row_tap : 2 - row_tap + amount,
                        2 - time_tap : 2 - time_tap + frame_count,
                        2 - col_tap : 2 - col_tap + columns,
                    ]
                )
    stacked = jnp.stack(windows, 0).reshape(27 * 3, amount * frame_count * columns)
    kernel = out_weight.reshape(27 * 3, out_weight.shape[4])
    summed = lax.dot_general(
        stacked, kernel, (((0,), (0,)), ((), ())), preferred_element_type=jnp.float32
    )
    return summed.reshape(amount, frame_count, columns, out_weight.shape[4])


def inner_back(padded, inner_weight, amount):
    frame_count = padded.shape[1]
    columns = padded.shape[2]
    channel_count = padded.shape[3]
    widened = jnp.pad(padded, ((0, 0), (0, 2), (1, 1), (0, 0)))
    summed = jnp.zeros((amount * frame_count * columns, inner_weight.shape[3]), jnp.float32)
    for time_tap in range(3):
        windows = []
        for row_tap in range(3):
            for col_tap in range(3):
                windows.append(
                    widened[
                        2 - row_tap : 2 - row_tap + amount,
                        2 - time_tap : 2 - time_tap + frame_count,
                        2 - col_tap : 2 - col_tap + columns,
                        :,
                    ]
                )
        joined = jnp.concatenate(windows, axis=3).reshape(
            amount * frame_count * columns, 9 * channel_count
        )
        kernel = jnp.transpose(inner_weight[time_tap], (0, 1, 3, 2)).reshape(
            9 * channel_count, inner_weight.shape[3]
        )
        summed = summed + jnp.dot(joined, kernel, preferred_element_type=jnp.float32)
    return summed.reshape(amount, frame_count, columns, inner_weight.shape[3])


def group_back(state_rows, slope_in, group_mean, inverse, group_gain, group_shift, cell_total):
    grouped = state_rows.astype(jnp.float32).reshape(state_rows.shape[:3] + (GROUPS, -1))
    gain_table = group_gain.reshape(GROUPS, -1)
    shift_table = group_shift.reshape(GROUPS, -1)
    normed_state = (grouped - group_mean[:, None]) * inverse[:, None]
    affine = normed_state * gain_table + shift_table
    upstream = slope_in.reshape(grouped.shape) * silu_slope(affine) * gain_table
    group_terms = lax.psum(
        (jnp.sum(upstream, axis=(0, 1, 2, 4)), jnp.sum(upstream * normed_state, axis=(0, 1, 2, 4))),
        "row",
    )
    first_part = group_terms[0] / cell_total
    second_part = group_terms[1] / cell_total
    state_grad = (upstream - first_part[:, None] - normed_state * second_part[:, None]) * inverse[
        :, None
    ]
    return state_grad.reshape(state_rows.shape).astype(jnp.bfloat16)


def per_device(
    frames,
    frame_owner,
    picks,
    patch_weight,
    patch_bias,
    norm_gain,
    head_weight,
    head_bias,
    head_out,
    hidden_state,
    group_gain,
    group_shift,
    out_weight,
    inner_weight,
):
    devices = lax.axis_size("row")
    position = lax.axis_index("row")
    per_frame = devices // FRAMES
    slot = position // per_frame
    height = frames.shape[1]
    strip = frames.shape[2]
    own_rows = hidden_state.shape[0]
    frame_width = hidden_state.shape[2]
    tokens = to_tokens(frames)
    embedded = jnp.dot(tokens, patch_weight, preferred_element_type=jnp.float32) + patch_bias
    centred = embedded - jnp.mean(embedded, axis=1, keepdims=True)
    inv_spread = lax.rsqrt(jnp.mean(centred * centred, axis=1, keepdims=True) + eps_norm)
    normed = centred * inv_spread
    slot_mask = (jnp.arange(FRAMES, dtype=jnp.int32) == slot).astype(jnp.float32)
    partial_pool = slot_mask[:, None] * jnp.sum(normed * norm_gain, axis=0)[None, :]
    grouped = hidden_state.reshape(own_rows, FRAMES, frame_width, GROUPS, -1)
    first_sum = jnp.sum(grouped, axis=(0, 1, 2, 4), dtype=jnp.float32)
    second_sum = jnp.sum(jnp.square(grouped.astype(jnp.float32)), axis=(0, 1, 2, 4))
    pooled_sum, first_total, second_total = lax.psum((partial_pool, first_sum, second_sum), "row")
    frame_tokens = height // PATCH * (strip * per_frame // PATCH)
    pooled = pooled_sum / frame_tokens
    head_full = head_weight.astype(jnp.float32)
    before = jnp.dot(pooled, head_full, precision=lax.Precision.HIGHEST) + head_bias
    pulled = jnp.dot(head_out * silu_slope(before), head_full.T, precision=lax.Precision.HIGHEST)
    picked = jnp.sum((picks[:, None] == frame_owner[None, :]).astype(jnp.float32), axis=0)
    slot_grad = jnp.dot(slot_mask * picked, pulled, precision=lax.Precision.HIGHEST)
    scaled = norm_gain * slot_grad
    token_grad = inv_spread * (
        scaled - jnp.mean(scaled) - normed * jnp.mean(scaled * normed, axis=1, keepdims=True)
    )
    patch_grad = lax.dot_general(
        token_grad.astype(jnp.bfloat16),
        patch_weight,
        (((1,), (1,)), ((), ())),
        preferred_element_type=jnp.float32,
    )
    pixel_local = from_tokens(patch_grad, height, strip).astype(jnp.bfloat16)
    arrived = lax.all_to_all(pixel_local, "row", split_axis=1, concat_axis=2, tiled=True)
    by_slot = arrived.reshape(3, own_rows, FRAMES, frame_width)
    owner_table = (frame_owner[:, None] == jnp.arange(FRAMES, dtype=jnp.int32)[None, :]).astype(
        jnp.bfloat16
    )
    ordered = jnp.einsum(
        "krbw,bf->krfw", by_slot, owner_table, preferred_element_type=jnp.float32
    ).astype(jnp.bfloat16)
    cell_total = own_rows * devices * FRAMES * frame_width * (hidden_state.shape[3] // GROUPS)
    group_mean = first_total / cell_total
    inverse = lax.rsqrt(second_total / cell_total - group_mean * group_mean + eps_norm)
    pixel_padded = extended(ordered, (("row", 1),), 1)
    slope_in = pixel_back(pixel_padded, out_weight, own_rows)
    state_grad = group_back(
        hidden_state, slope_in, group_mean, inverse, group_gain, group_shift, cell_total
    )
    grad_padded = extended(state_grad, (("row", 0),), 1)
    return inner_back(grad_padded, inner_weight, own_rows).astype(jnp.bfloat16)


def split_rows(row):
    high = row.astype(jnp.bfloat16).astype(jnp.float32)
    rest = row - high
    middle = rest.astype(jnp.bfloat16).astype(jnp.float32)
    low = rest - middle
    index = lax.broadcasted_iota(jnp.int32, (8, row.shape[1]), 0)
    stacked = jnp.where(
        index == 0, high, jnp.where(index == 1, middle, jnp.where(index == 2, low, 0.0))
    )
    return stacked.astype(jnp.bfloat16)


def fused_kernel(
    n,
    frames_any,
    owner_any,
    picks_any,
    patch_any,
    patch_bias_any,
    norm_gain_any,
    head_any,
    head_bias_any,
    head_out_any,
    hidden_any,
    group_gain_any,
    group_shift_any,
    out_weight_any,
    inner_any,
    out,
    frames,
    owner,
    picks,
    patch_bias,
    norm_gain,
    head_bias,
    head_out,
    group_gain,
    group_shift,
    out_weight,
    patch_w,
    head_w,
    hidden,
    inner_w,
    pixels,
    tokens,
    sent,
    arrived,
    by_frame,
    columns,
    band,
    slope,
    factor,
    normed_ref,
    turned,
    windows,
    sums_one,
    sums_two,
    local_sem,
    small_sem,
    halo_send,
    halo_recv,
    one_send,
    one_recv,
    pix_send,
    pix_recv,
    two_send,
    two_recv,
):
    me = lax.axis_index("row")
    strip, height = frames.shape[1], frames.shape[2]
    patch_rows = height // PATCH
    own = out.shape[0]
    wide = out.shape[3]
    channels = out.shape[4]
    line = FRAMES * wide
    per_group = channels // GROUPS
    cell_total = own * n * FRAMES * wide * per_group
    piece = 3 * strip
    half = arrived.shape[1]

    def peer(offset):
        return lax.rem(me + offset, n)

    loads = [
        pltpu.make_async_copy(hidden_any, hidden.at[pl.ds(1, own)], local_sem.at[0]),
        pltpu.make_async_copy(patch_any, patch_w, local_sem.at[1]),
        pltpu.make_async_copy(head_any, head_w, local_sem.at[2]),
        pltpu.make_async_copy(inner_any, inner_w, local_sem.at[3]),
    ]
    small = [
        pltpu.make_async_copy(source, target, small_sem.at[index])
        for index, (source, target) in enumerate(
            (
                (frames_any, frames),
                (owner_any, owner),
                (picks_any, picks),
                (patch_bias_any, patch_bias),
                (norm_gain_any, norm_gain),
                (head_bias_any, head_bias),
                (head_out_any, head_out),
                (group_gain_any, group_gain),
                (group_shift_any, group_shift),
                (out_weight_any, out_weight),
            )
        )
    ]
    small[0].start()
    loads[0].start()
    loads[1].start()
    for load in small[1:]:
        load.start()
    loads[2].start()
    loads[3].start()

    barrier = pltpu.get_barrier_semaphore()
    for offset in range(1, n):
        pl.semaphore_signal(barrier, inc=1, device_id={"row": peer(offset)}, device_id_type=MESH)

    small[0].wait()
    for colour in range(3):
        pixels[colour] = frames[colour].astype(jnp.float32).T
    tokens[...] = jnp.zeros_like(tokens)
    for colour in range(3):
        for line_in in range(PATCH):
            at = (colour * PATCH + line_in) * PATCH
            tokens[0:patch_rows, at : at + PATCH] = pixels[
                colour, pl.ds(line_in, patch_rows, stride=PATCH), :
            ]
    sent[...] = jnp.zeros_like(sent)

    loads[0].wait()
    first = jnp.zeros((1, channels), jnp.float32)
    second = jnp.zeros((1, channels), jnp.float32)
    for row in range(own):
        state = hidden[1 + row].reshape(line, channels).astype(jnp.float32)
        first = first + jnp.sum(state, axis=0, keepdims=True)
        second = second + jnp.sum(state * state, axis=0, keepdims=True)
    spot = lax.broadcasted_iota(jnp.int32, (2, channels), 0)
    sums_one[me] = jnp.where(spot == 0, first, second)

    for load in small[1:]:
        load.wait()
    loads[1].wait()
    embedded = (
        jnp.dot(
            tokens[...].astype(jnp.bfloat16), patch_w[...], preferred_element_type=jnp.float32
        )
        + patch_bias[...]
    )
    centred = embedded - jnp.mean(embedded, axis=1, keepdims=True)
    inv_spread = lax.rsqrt(jnp.mean(centred * centred, axis=1, keepdims=True) + eps_norm)
    normed = centred * inv_spread
    gain = norm_gain[...]
    pooled = jnp.sum((normed * gain)[0:patch_rows], axis=0, keepdims=True) / patch_rows
    pl.semaphore_wait(barrier, n - 1)

    def broadcast(buffer, send_sem, recv_sem):
        copies = []
        for offset in range(1, n):
            copy = pltpu.make_async_remote_copy(
                src_ref=buffer.at[me],
                dst_ref=buffer.at[me],
                send_sem=send_sem.at[offset],
                recv_sem=recv_sem.at[offset],
                device_id={"row": peer(offset)},
                device_id_type=MESH,
            )
            copy.start()
            copies.append(copy)
        return copies

    one_copies = broadcast(sums_one, one_send, one_recv)
    halo_copies = [
        pltpu.make_async_remote_copy(
            src_ref=hidden_any.at[pl.ds(own - 1, 1)],
            dst_ref=hidden.at[pl.ds(0, 1)],
            send_sem=halo_send.at[0],
            recv_sem=halo_recv.at[0],
            device_id={"row": peer(1)},
            device_id_type=MESH,
        ),
        pltpu.make_async_remote_copy(
            src_ref=hidden_any.at[pl.ds(0, 1)],
            dst_ref=hidden.at[pl.ds(own + 1, 1)],
            send_sem=halo_send.at[1],
            recv_sem=halo_recv.at[1],
            device_id={"row": peer(n - 1)},
            device_id_type=MESH,
        ),
    ]
    for copy in halo_copies:
        copy.start()

    loads[2].wait()
    before = (
        jnp.sum(
            jnp.dot(split_rows(pooled), head_w[...], preferred_element_type=jnp.float32),
            axis=0,
            keepdims=True,
        )
        + head_bias[...]
    )
    pulled = jnp.sum(
        lax.dot_general(
            split_rows(head_out[...] * silu_slope(before)),
            head_w[...],
            (((1,), (1,)), ((), ())),
            preferred_element_type=jnp.float32,
        ),
        axis=0,
        keepdims=True,
    )
    mine = owner[me]
    picked = jnp.float32(0.0)
    for pick in range(picks.shape[0]):
        picked = picked + jnp.where(picks[pick] == mine, jnp.float32(1.0), jnp.float32(0.0))
    scaled = gain * (picked * pulled)
    token_grad = inv_spread * (
        scaled
        - jnp.mean(scaled, axis=1, keepdims=True)
        - normed * jnp.mean(scaled * normed, axis=1, keepdims=True)
    )
    patch_grad = lax.dot_general(
        token_grad.astype(jnp.bfloat16),
        patch_w[...],
        (((1,), (1,)), ((), ())),
        preferred_element_type=jnp.float32,
    )
    patch_grad = patch_grad.astype(jnp.bfloat16).astype(jnp.float32)
    for line_in in range(PATCH):
        joined = jnp.concatenate(
            [
                patch_grad[:, (colour * PATCH + line_in) * PATCH : (colour * PATCH + line_in + 1) * PATCH]
                for colour in range(3)
            ],
            axis=1,
        )
        for patch_row in range(patch_rows):
            at = 2 + patch_row * PATCH + line_in
            sent[at, :, 0:piece] = joined[patch_row : patch_row + 1]
            if at >= half:
                sent[at - half, :, 64 : 64 + piece] = joined[patch_row : patch_row + 1]

    pix_copies = []
    for offset in range(1, n):
        target = peer(offset)
        copy = pltpu.make_async_remote_copy(
            src_ref=sent.at[pl.ds(target * own, half)],
            dst_ref=arrived.at[me],
            send_sem=pix_send.at[offset],
            recv_sem=pix_recv.at[offset],
            device_id={"row": target},
            device_id_type=MESH,
        )
        copy.start()
        pix_copies.append(copy)
    arrived[me] = sent[pl.ds(me * own, half)]

    column = lax.broadcasted_iota(jnp.int32, (wide, channels), 0)
    for row_tap in range(3):
        for time_tap in range(3):
            taps = [out_weight[time_tap, row_tap, col_tap].astype(jnp.float32) for col_tap in range(3)]
            for colour in range(3):
                at = ((row_tap * 3 + time_tap) * 3 + colour) * wide
                spread = [
                    jnp.broadcast_to(tap[colour : colour + 1], (wide, channels)) for tap in taps
                ]
                for w in range(wide):
                    block = jnp.where(
                        column == w + 1,
                        spread[0],
                        jnp.where(
                            column == w, spread[1], jnp.where(column == w - 1, spread[2], 0.0)
                        ),
                    )
                    band[at : at + wide, w * channels : (w + 1) * channels] = block.astype(
                        jnp.bfloat16
                    )
    depth = band.shape[0]
    if depth > 27 * wide:
        band[27 * wide :, :] = jnp.zeros((depth - 27 * wide, wide * channels), jnp.bfloat16)
    columns[...] = jnp.zeros_like(columns)
    by_frame[...] = jnp.zeros_like(by_frame)

    group_row = lax.broadcasted_iota(jnp.int32, (channels, channels), 0) // per_group
    group_col = lax.broadcasted_iota(jnp.int32, (channels, channels), 1) // per_group
    same_group = (group_row == group_col).astype(jnp.float32)

    def group_sums(buffer):
        total = buffer[0]
        for slot in range(1, n):
            total = total + buffer[slot]
        return jnp.dot(total, same_group, precision=lax.Precision.HIGHEST) / cell_total

    for copy in one_copies:
        copy.wait()
    means = group_sums(sums_one)
    group_mean = means[0:1]
    inverse = lax.rsqrt(means[1:2] - group_mean * group_mean + eps_norm)
    for copy in halo_copies:
        copy.wait()
    for row in range(own + 2):
        state = hidden[row].reshape(line, channels).astype(jnp.float32)
        normed_state = (state - group_mean) * inverse
        normed_ref[row * line : (row + 1) * line] = normed_state
        affine = normed_state * group_gain[...] + group_shift[...]
        factor[row * line : (row + 1) * line] = silu_slope(affine) * group_gain[...]

    slot_of = []
    for frame in range(FRAMES):
        found = jnp.int32(0)
        for slot in range(n):
            found = jnp.where(owner[slot] == frame, jnp.int32(slot), found)
        slot_of.append(found)

    for copy in pix_copies:
        copy.wait()
    for frame in range(FRAMES):
        for row in range(half):
            by_frame[row, frame : frame + 1, :] = arrived[slot_of[frame], row]
    for row_tap in range(3):
        for time_tap in range(3):
            at = (row_tap * 3 + time_tap) * piece
            for row in range(own + 2):
                source = row - row_tap + 2
                lane = source // half * 64
                columns[row * FRAMES : (row + 1) * FRAMES, at : at + piece] = by_frame[
                    source % half, 2 - time_tap : 2 - time_tap + FRAMES, lane : lane + piece
                ]
    left = columns[...].astype(jnp.bfloat16)
    for w in range(0, wide, 2):
        both = jnp.dot(
            left,
            band[:, w * channels : (w + 2) * channels],
            preferred_element_type=jnp.float32,
        )
        for side in range(2):
            slope[pl.ds(w + side, (own + 2) * FRAMES, stride=wide), :] = both[
                :, side * channels : (side + 1) * channels
            ]

    first = jnp.zeros((1, channels), jnp.float32)
    second = jnp.zeros((1, channels), jnp.float32)
    for row in range(own + 2):
        part = pl.ds(row * line, line)
        upstream = slope[part] * factor[part]
        slope[part] = upstream
        if 1 <= row <= own:
            first = first + jnp.sum(upstream, axis=0, keepdims=True)
            second = second + jnp.sum(upstream * normed_ref[part], axis=0, keepdims=True)
    sums_two[me] = jnp.where(spot == 0, first, second)
    two_copies = broadcast(sums_two, two_send, two_recv)

    loads[3].wait()
    for row_tap in range(3):
        for col_tap in range(3):
            part = pl.ds(col_tap * channels, channels)
            for time_tap in range(3):
                block = inner_w[time_tap, row_tap, col_tap].T
                turned[row_tap, 2 - time_tap, part, 0:channels] = block
                turned[row_tap, 3 - time_tap, part, channels:] = block
            empty = jnp.zeros((channels, channels), jnp.bfloat16)
            turned[row_tap, 3, part, 0:channels] = empty
            turned[row_tap, 0, part, channels:] = empty
    windows[:, FRAMES // 2] = jnp.zeros((own + 2, 2, wide, 3 * channels), jnp.bfloat16)

    for copy in two_copies:
        copy.wait()
    parts = group_sums(sums_two)
    position = lax.rem(lax.broadcasted_iota(jnp.int32, (line, channels), 0), wide)
    for row in range(own + 2):
        part = pl.ds(row * line, line)
        state_grad = (slope[part] - parts[0:1] - normed_ref[part] * parts[1:2]) * inverse
        if row == 0:
            state_grad = jnp.where(me > 0, state_grad, 0.0)
        if row == own + 1:
            state_grad = jnp.where(me < n - 1, state_grad, 0.0)
        after = jnp.where(position == wide - 1, 0.0, pltpu.roll(state_grad, line - 1, 0))
        earlier = jnp.where(position == 0, 0.0, pltpu.roll(state_grad, 1, 0))
        for col_tap, shifted in enumerate((after, state_grad, earlier)):
            windows[row, 0 : FRAMES // 2, :, :, col_tap * channels : (col_tap + 1) * channels] = (
                shifted.astype(jnp.bfloat16).reshape(FRAMES // 2, 2, wide, channels)
            )
    rows = own * line // 2
    taken = jnp.concatenate(
        [
            windows[
                2 - row_tap : 2 - row_tap + own, ahead // 2 : ahead // 2 + FRAMES // 2, ahead % 2
            ].reshape(rows, 3 * channels)
            for row_tap in range(3)
            for ahead in range(4)
        ],
        axis=1,
    )
    summed = jnp.dot(
        taken,
        turned[...].reshape(12 * 3 * channels, 2 * channels),
        preferred_element_type=jnp.float32,
    )
    for side in range(2):
        out[:, :, side] = (
            summed[:, side * channels : (side + 1) * channels]
            .reshape(own, FRAMES // 2, wide, channels)
            .astype(jnp.bfloat16)
        )


def one_frame_each(
    frames,
    frame_owner,
    picks,
    patch_weight,
    patch_bias,
    norm_gain,
    head_weight,
    head_bias,
    head_out,
    hidden_state,
    group_gain,
    group_shift,
    out_weight,
    inner_weight,
):
    n = lax.axis_size("row")
    own, frame_count, wide, channels = hidden_state.shape
    height, strip = frames.shape[1:]
    pix, width = patch_weight.shape
    depth = -(-27 * wide // 128) * 128
    cells = (own + 2) * frame_count * wide
    f32, bf16 = jnp.float32, jnp.bfloat16
    vmem = pl.BlockSpec(memory_space=pltpu.VMEM)
    dma = pltpu.SemaphoreType.DMA
    return pl.pallas_call(
        functools.partial(fused_kernel, n),
        out_shape=jax.ShapeDtypeStruct((own, frame_count // 2, 2, wide, channels), bf16),
        in_specs=[pl.BlockSpec(memory_space=pltpu.HBM)] * 14,
        out_specs=vmem,
        scratch_shapes=[
            pltpu.VMEM((3, strip, height), bf16),
            pltpu.SMEM(frame_owner.shape, jnp.int32),
            pltpu.SMEM(picks.shape, jnp.int32),
            pltpu.VMEM((1, width), f32),
            pltpu.VMEM((1, width), f32),
            pltpu.VMEM((1, width), f32),
            pltpu.VMEM((1, width), f32),
            pltpu.VMEM((1, channels), f32),
            pltpu.VMEM((1, channels), f32),
            pltpu.VMEM(out_weight.shape, bf16),
            pltpu.VMEM((pix, width), bf16),
            pltpu.VMEM(head_weight.shape, bf16),
            pltpu.VMEM((own + 2, frame_count, wide, channels), bf16),
            pltpu.VMEM(inner_weight.shape, bf16),
            pltpu.VMEM(frames.shape, f32),
            pltpu.VMEM((-(-(height // PATCH) // 8) * 8, pix), f32),
            pltpu.VMEM((height + 4, 1, 128), f32),
            pltpu.VMEM((n, (own + 5) // 2, 1, 128), f32),
            pltpu.VMEM(((own + 5) // 2, frame_count + 8, 128), f32),
            pltpu.VMEM(((own + 2) * frame_count, depth), f32),
            pltpu.VMEM((depth, wide * channels), bf16),
            pltpu.VMEM((cells, channels), f32),
            pltpu.VMEM((cells, channels), f32),
            pltpu.VMEM((cells, channels), f32),
            pltpu.VMEM((3, 4, 3 * channels, 2 * channels), bf16),
            pltpu.VMEM((own + 2, frame_count // 2 + 1, 2, wide, 3 * channels), bf16),
            pltpu.VMEM((n, 2, channels), f32),
            pltpu.VMEM((n, 2, channels), f32),
            dma((4,)),
            dma((10,)),
            dma((2,)),
            dma((2,)),
            dma((n,)),
            dma((n,)),
            dma((n,)),
            dma((n,)),
            dma((n,)),
            dma((n,)),
        ],
        compiler_params=pltpu.CompilerParams(
            collective_id=0, has_side_effects=True
        ),
    )(
        frames.transpose(0, 2, 1),
        frame_owner,
        picks,
        patch_weight,
        patch_bias[None],
        norm_gain[None],
        head_weight,
        head_bias[None],
        head_out[None],
        hidden_state,
        group_gain[None],
        group_shift[None],
        out_weight,
        inner_weight,
    ).reshape(hidden_state.shape)


def solution(mesh):
    body = one_frame_each if mesh.shape["row"] == FRAMES else per_device
    return jax.shard_map(
        body,
        mesh=mesh,
        in_specs=(
            P(None, None, ("clip", "row")),
            P("clip"),
            P("clip"),
            P(),
            P(),
            P(),
            P(),
            P(),
            P(),
            P(("clip", "row"), None, None, None),
            P(),
            P(),
            P(),
            P(),
        ),
        out_specs=P(("clip", "row"), None, None, None),
        check_vma=False,
    )
```

profile of v0, /device:TPU:0, one launch (start us, length us, event | category | flops | bytes accessed | tf_op | source)
XLA Modules:
  0.0 21.7 jit_solution(12115572018678033787)
XLA Ops:
  0.0 20.1 %shard_map.136 = bf16[3,8,2,16,128]{4,3,2,1,0:T(8,128)(2,1)} custom-call(bf16[3,16,48]{2,1,0:T(8,128)(2,1)} %bitcast.9, s32[16]{0:T(128)} %owner_any.1, s32[8]{0:T(128)} %picks_any.1, bf16[768,1024]{1,0:T(8,128)(2,1)} %patch_any.1, f32[1,1024]{1,0:T(1,128)} %bitcast.10, f32[1,1024]{1,0:T(1,128)} %bitcast.11, bf16[1024,1024]{1,0:T(8,128)(2,1)} %head_any.1, ...), custom_call_target="tpu_custom_call" | custom-call | tf_op jit(solution)/shard_map/pallas_call | solution.py:626
  20.1 1.6 %copy.16 = bf16[3,16,16,128]{3,2,1,0:T(8,128)(2,1)} copy(bf16[3,16,16,128]{3,2,1,0:T(8,128)(2,1)} %bitcast.8) | data formatting | bytes 393216
where the time goes:
time: 21.9 us; the launch traced here: 21.7 us
  Pallas kernels  20.1 us (92%)
  local copies, waits for them, and re-layouts  1.62 us (7%)
    pallas_call x1, Pallas kernels, one_frame_each(): pl.pallas_call(functools.partial(fused_kernel, n), out_shape=jax.ShapeDty...  20.1 us
    unnamed x1, local copies, waits for them, and re-layouts  1.62 us

commit v1 on v0

--- a/solution.py
+++ b/solution.py
@@ -272,7 +272,19 @@
     half = arrived.shape[1]
 
     def peer(offset):
-        return lax.rem(me + offset, n)
+        target = me
+        step = 1
+        while step < n:
+            if offset // step % 2:
+                target = target + step * (1 - 2 * lax.rem(lax.div(me, step), 2))
+            step *= 2
+        return target
+
+    farthest_first = range(n - 1, 0, -1)
+
+    barrier = pltpu.get_barrier_semaphore()
+    for offset in farthest_first:
+        pl.semaphore_signal(barrier, inc=1, device_id={"row": peer(offset)}, device_id_type=MESH)
 
     loads = [
         pltpu.make_async_copy(hidden_any, hidden.at[pl.ds(1, own)], local_sem.at[0]),
@@ -305,10 +317,6 @@
     loads[2].start()
     loads[3].start()
 
-    barrier = pltpu.get_barrier_semaphore()
-    for offset in range(1, n):
-        pl.semaphore_signal(barrier, inc=1, device_id={"row": peer(offset)}, device_id_type=MESH)
-
     small[0].wait()
     for colour in range(3):
         pixels[colour] = frames[colour].astype(jnp.float32).T
@@ -345,11 +353,61 @@
     normed = centred * inv_spread
     gain = norm_gain[...]
     pooled = jnp.sum((normed * gain)[0:patch_rows], axis=0, keepdims=True) / patch_rows
+    loads[2].wait()
+    before = (
+        jnp.sum(
+            jnp.dot(split_rows(pooled), head_w[...], preferred_element_type=jnp.float32),
+            axis=0,
+            keepdims=True,
+        )
+        + head_bias[...]
+    )
+    pulled = jnp.sum(
+        lax.dot_general(
+            split_rows(head_out[...] * silu_slope(before)),
+            head_w[...],
+            (((1,), (1,)), ((), ())),
+            preferred_element_type=jnp.float32,
+        ),
+        axis=0,
+        keepdims=True,
+    )
+    mine = owner[me]
+    picked = jnp.float32(0.0)
+    for pick in range(picks.shape[0]):
+        picked = picked + jnp.where(picks[pick] == mine, jnp.float32(1.0), jnp.float32(0.0))
+    scaled = gain * (picked * pulled)
+    token_grad = inv_spread * (
+        scaled
+        - jnp.mean(scaled, axis=1, keepdims=True)
+        - normed * jnp.mean(scaled * normed, axis=1, keepdims=True)
+    )
+    patch_grad = lax.dot_general(
+        token_grad.astype(jnp.bfloat16),
+        patch_w[...],
+        (((1,), (1,)), ((), ())),
+        preferred_element_type=jnp.float32,
+    )
+    patch_grad = patch_grad.astype(jnp.bfloat16).astype(jnp.float32)
+    for line_in in range(PATCH):
+        joined = jnp.concatenate(
+            [
+                patch_grad[:, (colour * PATCH + line_in) * PATCH : (colour * PATCH + line_in + 1) * PATCH]
+                for colour in range(3)
+            ],
+            axis=1,
+        )
+        for patch_row in range(patch_rows):
+            at = 2 + patch_row * PATCH + line_in
+            sent[at, :, 0:piece] = joined[patch_row : patch_row + 1]
+            if at >= half:
+                sent[at - half, :, 64 : 64 + piece] = joined[patch_row : patch_row + 1]
+
     pl.semaphore_wait(barrier, n - 1)
 
     def broadcast(buffer, send_sem, recv_sem):
         copies = []
-        for offset in range(1, n):
+        for offset in farthest_first:
             copy = pltpu.make_async_remote_copy(
                 src_ref=buffer.at[me],
                 dst_ref=buffer.at[me],
@@ -362,80 +420,8 @@
             copies.append(copy)
         return copies
 
-    one_copies = broadcast(sums_one, one_send, one_recv)
-    halo_copies = [
-        pltpu.make_async_remote_copy(
-            src_ref=hidden_any.at[pl.ds(own - 1, 1)],
-            dst_ref=hidden.at[pl.ds(0, 1)],
-            send_sem=halo_send.at[0],
-            recv_sem=halo_recv.at[0],
-            device_id={"row": peer(1)},
-            device_id_type=MESH,
-        ),
-        pltpu.make_async_remote_copy(
-            src_ref=hidden_any.at[pl.ds(0, 1)],
-            dst_ref=hidden.at[pl.ds(own + 1, 1)],
-            send_sem=halo_send.at[1],
-            recv_sem=halo_recv.at[1],
-            device_id={"row": peer(n - 1)},
-            device_id_type=MESH,
-        ),
-    ]
-    for copy in halo_copies:
-        copy.start()
-
-    loads[2].wait()
-    before = (
-        jnp.sum(
-            jnp.dot(split_rows(pooled), head_w[...], preferred_element_type=jnp.float32),
-            axis=0,
-            keepdims=True,
-        )
-        + head_bias[...]
-    )
-    pulled = jnp.sum(
-        lax.dot_general(
-            split_rows(head_out[...] * silu_slope(before)),
-            head_w[...],
-            (((1,), (1,)), ((), ())),
-            preferred_element_type=jnp.float32,
-        ),
-        axis=0,
-        keepdims=True,
-    )
-    mine = owner[me]
-    picked = jnp.float32(0.0)
-    for pick in range(picks.shape[0]):
-        picked = picked + jnp.where(picks[pick] == mine, jnp.float32(1.0), jnp.float32(0.0))
-    scaled = gain * (picked * pulled)
-    token_grad = inv_spread * (
-        scaled
-        - jnp.mean(scaled, axis=1, keepdims=True)
-        - normed * jnp.mean(scaled * normed, axis=1, keepdims=True)
-    )
-    patch_grad = lax.dot_general(
-        token_grad.astype(jnp.bfloat16),
-        patch_w[...],
-        (((1,), (1,)), ((), ())),
-        preferred_element_type=jnp.float32,
-    )
-    patch_grad = patch_grad.astype(jnp.bfloat16).astype(jnp.float32)
-    for line_in in range(PATCH):
-        joined = jnp.concatenate(
-            [
-                patch_grad[:, (colour * PATCH + line_in) * PATCH : (colour * PATCH + line_in + 1) * PATCH]
-                for colour in range(3)
-            ],
-            axis=1,
-        )
-        for patch_row in range(patch_rows):
-            at = 2 + patch_row * PATCH + line_in
-            sent[at, :, 0:piece] = joined[patch_row : patch_row + 1]
-            if at >= half:
-                sent[at - half, :, 64 : 64 + piece] = joined[patch_row : patch_row + 1]
-
     pix_copies = []
-    for offset in range(1, n):
+    for offset in farthest_first:
         target = peer(offset)
         copy = pltpu.make_async_remote_copy(
             src_ref=sent.at[pl.ds(target * own, half)],
@@ -447,6 +433,40 @@
         )
         copy.start()
         pix_copies.append(copy)
+    one_copies = broadcast(sums_one, one_send, one_recv)
+    to_right = pltpu.make_async_remote_copy(
+        src_ref=hidden_any.at[pl.ds(own - 1, 1)],
+        dst_ref=hidden.at[pl.ds(0, 1)],
+        send_sem=halo_send.at[0],
+        recv_sem=halo_recv.at[0],
+        device_id={"row": lax.rem(me + 1, n)},
+        device_id_type=MESH,
+    )
+    to_left = pltpu.make_async_remote_copy(
+        src_ref=hidden_any.at[pl.ds(0, 1)],
+        dst_ref=hidden.at[pl.ds(own + 1, 1)],
+        send_sem=halo_send.at[1],
+        recv_sem=halo_recv.at[1],
+        device_id={"row": lax.rem(me + n - 1, n)},
+        device_id_type=MESH,
+    )
+
+    @pl.when(me < n - 1)
+    def _():
+        to_right.start()
+
+    @pl.when(me > 0)
+    def _():
+        to_left.start()
+
+    @pl.when(me == 0)
+    def _():
+        hidden[0] = jnp.zeros(hidden.shape[1:], hidden.dtype)
+
+    @pl.when(me == n - 1)
+    def _():
+        hidden[own + 1] = jnp.zeros(hidden.shape[1:], hidden.dtype)
+
     arrived[me] = sent[pl.ds(me * own, half)]
 
     column = lax.broadcasted_iota(jnp.int32, (wide, channels), 0)
@@ -490,8 +510,17 @@
     means = group_sums(sums_one)
     group_mean = means[0:1]
     inverse = lax.rsqrt(means[1:2] - group_mean * group_mean + eps_norm)
-    for copy in halo_copies:
-        copy.wait()
+
+    @pl.when(me < n - 1)
+    def _():
+        to_right.wait_send()
+        to_left.wait_recv()
+
+    @pl.when(me > 0)
+    def _():
+        to_left.wait_send()
+        to_right.wait_recv()
+
     for row in range(own + 2):
         state = hidden[row].reshape(line, channels).astype(jnp.float32)
         normed_state = (state - group_mean) * inverse

time: 21.9 us -> 21.2 us (0.968)
  Pallas kernels: 20.1 us -> 19.4 us
    pallas_call x1, Pallas kernels: 20.1 us -> 19.4 us  [one_frame_each(): pl.pallas_call(functools.partial(fused_kernel, n), out_shape=jax.ShapeDty...]
where the time goes in v1:
time: 21.2 us; the launch traced here: 21 us
  Pallas kernels  19.4 us (92%)
  local copies, waits for them, and re-layouts  1.62 us (8%)
    pallas_call x1, Pallas kernels, one_frame_each(): pl.pallas_call(functools.partial(fused_kernel, n), out_shape=jax.ShapeDty...  19.4 us
    unnamed x1, local copies, waits for them, and re-layouts  1.62 us

profile of v1, /device:TPU:0, one launch (start us, length us, event | category | flops | bytes accessed | tf_op | source)
XLA Modules:
  0.0 21.0 jit_solution(6628955515393356260)
XLA Ops:
  0.0 19.4 %shard_map.136 = bf16[3,8,2,16,128]{4,3,2,1,0:T(8,128)(2,1)} custom-call(bf16[3,16,48]{2,1,0:T(8,128)(2,1)} %bitcast.9, s32[16]{0:T(128)} %owner_any.1, s32[8]{0:T(128)} %picks_any.1, bf16[768,1024]{1,0:T(8,128)(2,1)} %patch_any.1, f32[1,1024]{1,0:T(1,128)} %bitcast.10, f32[1,1024]{1,0:T(1,128)} %bitcast.11, bf16[1024,1024]{1,0:T(8,128)(2,1)} %head_any.1, ...), custom_call_target="tpu_custom_call" | custom-call | tf_op jit(solution)/shard_map/pallas_call | solution.py:655
  19.4 1.6 %copy.16 = bf16[3,16,16,128]{3,2,1,0:T(8,128)(2,1)} copy(bf16[3,16,16,128]{3,2,1,0:T(8,128)(2,1)} %bitcast.8) | data formatting | bytes 393216

commit v2 on v1

--- a/solution.py
+++ b/solution.py
@@ -219,16 +219,15 @@
     group_shift_any,
     out_weight_any,
     inner_any,
-    out,
+    ready,
+    normed_ref,
+    terms,
+    turned,
     frames,
     owner,
     picks,
-    patch_bias,
-    norm_gain,
-    head_bias,
-    head_out,
-    group_gain,
-    group_shift,
+    wide_rows,
+    group_rows,
     out_weight,
     patch_w,
     head_w,
@@ -243,28 +242,20 @@
     band,
     slope,
     factor,
-    normed_ref,
-    turned,
-    windows,
     sums_one,
     sums_two,
     local_sem,
-    small_sem,
     halo_send,
     halo_recv,
-    one_send,
-    one_recv,
-    pix_send,
-    pix_recv,
-    two_send,
-    two_recv,
+    send_sem,
+    recv_sem,
 ):
     me = lax.axis_index("row")
     strip, height = frames.shape[1], frames.shape[2]
     patch_rows = height // PATCH
-    own = out.shape[0]
-    wide = out.shape[3]
-    channels = out.shape[4]
+    own = hidden.shape[0] - 2
+    wide = hidden.shape[2]
+    channels = hidden.shape[3]
     line = FRAMES * wide
     per_group = channels // GROUPS
     cell_total = own * n * FRAMES * wide * per_group
@@ -286,38 +277,66 @@
     for offset in farthest_first:
         pl.semaphore_signal(barrier, inc=1, device_id={"row": peer(offset)}, device_id_type=MESH)
 
-    loads = [
-        pltpu.make_async_copy(hidden_any, hidden.at[pl.ds(1, own)], local_sem.at[0]),
-        pltpu.make_async_copy(patch_any, patch_w, local_sem.at[1]),
-        pltpu.make_async_copy(head_any, head_w, local_sem.at[2]),
-        pltpu.make_async_copy(inner_any, inner_w, local_sem.at[3]),
+    load_frames = pltpu.make_async_copy(frames_any, frames, local_sem.at[0])
+    load_hidden = pltpu.make_async_copy(hidden_any, hidden.at[pl.ds(1, own)], local_sem.at[1])
+    load_patch = pltpu.make_async_copy(patch_any, patch_w, local_sem.at[2])
+    load_head = pltpu.make_async_copy(head_any, head_w, local_sem.at[3])
+    load_inner = pltpu.make_async_copy(inner_any, inner_w, local_sem.at[4])
+    load_out = pltpu.make_async_copy(out_weight_any, out_weight, local_sem.at[5])
+    load_owner = pltpu.make_async_copy(owner_any, owner, local_sem.at[6])
+    load_picks = pltpu.make_async_copy(picks_any, picks, local_sem.at[7])
+    load_wide = [
+        pltpu.make_async_copy(source, wide_rows.at[index], local_sem.at[8])
+        for index, source in enumerate((patch_bias_any, norm_gain_any, head_bias_any, head_out_any))
     ]
-    small = [
-        pltpu.make_async_copy(source, target, small_sem.at[index])
-        for index, (source, target) in enumerate(
-            (
-                (frames_any, frames),
-                (owner_any, owner),
-                (picks_any, picks),
-                (patch_bias_any, patch_bias),
-                (norm_gain_any, norm_gain),
-                (head_bias_any, head_bias),
-                (head_out_any, head_out),
-                (group_gain_any, group_gain),
-                (group_shift_any, group_shift),
-                (out_weight_any, out_weight),
-            )
-        )
+    load_group = [
+        pltpu.make_async_copy(source, group_rows.at[index], local_sem.at[9])
+        for index, source in enumerate((group_gain_any, group_shift_any))
     ]
-    small[0].start()
-    loads[0].start()
-    loads[1].start()
-    for load in small[1:]:
+    load_frames.start()
+    load_hidden.start()
+    load_patch.start()
+    for load in load_wide + load_group:
         load.start()
-    loads[2].start()
-    loads[3].start()
-
-    small[0].wait()
+    load_owner.start()
+    load_picks.start()
+    load_out.start()
+    load_head.start()
+    load_inner.start()
+
+    group_row = lax.broadcasted_iota(jnp.int32, (channels, channels), 0) // per_group
+    group_col = lax.broadcasted_iota(jnp.int32, (channels, channels), 1) // per_group
+    same_group = (group_row == group_col).astype(jnp.bfloat16)
+    eight = lax.broadcasted_iota(jnp.int32, (8, channels), 0)
+    spot = lax.broadcasted_iota(jnp.int32, (2, channels), 0)
+
+    def group_sums(first, second):
+        part = lax.rem(eight, 4)
+        row = jnp.where(eight < 4, first, second)
+        high = row.astype(jnp.bfloat16).astype(jnp.float32)
+        rest = row - high
+        middle = rest.astype(jnp.bfloat16).astype(jnp.float32)
+        stacked = jnp.where(
+            part == 0, high, jnp.where(part == 1, middle, jnp.where(part == 2, rest - middle, 0.0))
+        )
+        summed = jnp.dot(
+            stacked.astype(jnp.bfloat16), same_group, preferred_element_type=jnp.float32
+        )
+        return (
+            jnp.sum(summed[0:4], axis=0, keepdims=True),
+            jnp.sum(summed[4:8], axis=0, keepdims=True),
+        )
+
+    def over_devices(buffer):
+        blocks = [buffer[slot] for slot in range(n)]
+        while len(blocks) > 1:
+            blocks = [
+                blocks[at] + blocks[at + 1] if at + 1 < len(blocks) else blocks[at]
+                for at in range(0, len(blocks), 2)
+            ]
+        return blocks[0]
+
+    load_frames.wait()
     for colour in range(3):
         pixels[colour] = frames[colour].astype(jnp.float32).T
     tokens[...] = jnp.zeros_like(tokens)
@@ -329,42 +348,45 @@
             ]
     sent[...] = jnp.zeros_like(sent)
 
-    loads[0].wait()
+    load_hidden.wait()
     first = jnp.zeros((1, channels), jnp.float32)
     second = jnp.zeros((1, channels), jnp.float32)
     for row in range(own):
         state = hidden[1 + row].reshape(line, channels).astype(jnp.float32)
         first = first + jnp.sum(state, axis=0, keepdims=True)
         second = second + jnp.sum(state * state, axis=0, keepdims=True)
-    spot = lax.broadcasted_iota(jnp.int32, (2, channels), 0)
+    first, second = group_sums(first, second)
     sums_one[me] = jnp.where(spot == 0, first, second)
 
-    for load in small[1:]:
-        load.wait()
-    loads[1].wait()
+    pltpu.make_async_copy(wide_rows, wide_rows, local_sem.at[8]).wait()
+    pltpu.make_async_copy(group_rows, group_rows, local_sem.at[9]).wait()
+    load_owner.wait()
+    load_picks.wait()
+    load_out.wait()
+    load_patch.wait()
     embedded = (
         jnp.dot(
             tokens[...].astype(jnp.bfloat16), patch_w[...], preferred_element_type=jnp.float32
         )
-        + patch_bias[...]
+        + wide_rows[0]
     )
     centred = embedded - jnp.mean(embedded, axis=1, keepdims=True)
     inv_spread = lax.rsqrt(jnp.mean(centred * centred, axis=1, keepdims=True) + eps_norm)
     normed = centred * inv_spread
-    gain = norm_gain[...]
+    gain = wide_rows[1]
     pooled = jnp.sum((normed * gain)[0:patch_rows], axis=0, keepdims=True) / patch_rows
-    loads[2].wait()
+    load_head.wait()
     before = (
         jnp.sum(
             jnp.dot(split_rows(pooled), head_w[...], preferred_element_type=jnp.float32),
             axis=0,
             keepdims=True,
         )
-        + head_bias[...]
+        + wide_rows[2]
     )
     pulled = jnp.sum(
         lax.dot_general(
-            split_rows(head_out[...] * silu_slope(before)),
+            split_rows(wide_rows[3] * silu_slope(before)),
             head_w[...],
             (((1,), (1,)), ((), ())),
             preferred_element_type=jnp.float32,
@@ -405,35 +427,36 @@
 
     pl.semaphore_wait(barrier, n - 1)
 
-    def broadcast(buffer, send_sem, recv_sem):
-        copies = []
+    def broadcast(buffer, kind):
         for offset in farthest_first:
-            copy = pltpu.make_async_remote_copy(
+            pltpu.make_async_remote_copy(
                 src_ref=buffer.at[me],
                 dst_ref=buffer.at[me],
-                send_sem=send_sem.at[offset],
-                recv_sem=recv_sem.at[offset],
+                send_sem=send_sem.at[kind],
+                recv_sem=recv_sem.at[kind],
                 device_id={"row": peer(offset)},
                 device_id_type=MESH,
-            )
-            copy.start()
-            copies.append(copy)
-        return copies
-
-    pix_copies = []
+            ).start()
+
+    def from_peers(buffer, kind):
+        others = buffer.at[pl.ds(0, n - 1)]
+        pltpu.make_async_copy(others, others, recv_sem.at[kind]).wait()
+
+    def to_peers(buffer, kind):
+        others = buffer.at[pl.ds(0, n - 1)]
+        pltpu.make_async_copy(others, others, send_sem.at[kind]).wait()
+
     for offset in farthest_first:
         target = peer(offset)
-        copy = pltpu.make_async_remote_copy(
+        pltpu.make_async_remote_copy(
             src_ref=sent.at[pl.ds(target * own, half)],
             dst_ref=arrived.at[me],
-            send_sem=pix_send.at[offset],
-            recv_sem=pix_recv.at[offset],
+            send_sem=send_sem.at[1],
+            recv_sem=recv_sem.at[1],
             device_id={"row": target},
             device_id_type=MESH,
-        )
-        copy.start()
-        pix_copies.append(copy)
-    one_copies = broadcast(sums_one, one_send, one_recv)
+        ).start()
+    broadcast(sums_one, 0)
     to_right = pltpu.make_async_remote_copy(
         src_ref=hidden_any.at[pl.ds(own - 1, 1)],
         dst_ref=hidden.at[pl.ds(0, 1)],
@@ -495,39 +518,6 @@
     columns[...] = jnp.zeros_like(columns)
     by_frame[...] = jnp.zeros_like(by_frame)
 
-    group_row = lax.broadcasted_iota(jnp.int32, (channels, channels), 0) // per_group
-    group_col = lax.broadcasted_iota(jnp.int32, (channels, channels), 1) // per_group
-    same_group = (group_row == group_col).astype(jnp.float32)
-
-    def group_sums(buffer):
-        total = buffer[0]
-        for slot in range(1, n):
-            total = total + buffer[slot]
-        return jnp.dot(total, same_group, precision=lax.Precision.HIGHEST) / cell_total
-
-    for copy in one_copies:
-        copy.wait()
-    means = group_sums(sums_one)
-    group_mean = means[0:1]
-    inverse = lax.rsqrt(means[1:2] - group_mean * group_mean + eps_norm)
-
-    @pl.when(me < n - 1)
-    def _():
-        to_right.wait_send()
-        to_left.wait_recv()
-
-    @pl.when(me > 0)
-    def _():
-        to_left.wait_send()
-        to_right.wait_recv()
-
-    for row in range(own + 2):
-        state = hidden[row].reshape(line, channels).astype(jnp.float32)
-        normed_state = (state - group_mean) * inverse
-        normed_ref[row * line : (row + 1) * line] = normed_state
-        affine = normed_state * group_gain[...] + group_shift[...]
-        factor[row * line : (row + 1) * line] = silu_slope(affine) * group_gain[...]
-
     slot_of = []
     for frame in range(FRAMES):
         found = jnp.int32(0)
@@ -535,21 +525,40 @@
             found = jnp.where(owner[slot] == frame, jnp.int32(slot), found)
         slot_of.append(found)
 
-    for copy in pix_copies:
-        copy.wait()
-    for frame in range(FRAMES):
-        for row in range(half):
-            by_frame[row, frame : frame + 1, :] = arrived[slot_of[frame], row]
-    for row_tap in range(3):
-        for time_tap in range(3):
-            at = (row_tap * 3 + time_tap) * piece
-            for row in range(own + 2):
+    from_peers(sums_one, 0)
+    from_peers(arrived, 1)
+    means = over_devices(sums_one) / cell_total
+    group_mean = means[0:1]
+    inverse = lax.rsqrt(means[1:2] - group_mean * group_mean + eps_norm)
+    group_gain = group_rows[0]
+    group_shift = group_rows[1]
+
+    def state_terms(row):
+        state = hidden[row].reshape(line, channels).astype(jnp.float32)
+        normed_state = (state - group_mean) * inverse
+        normed_ref[row * line : (row + 1) * line] = normed_state
+        affine = normed_state * group_gain + group_shift
+        factor[row * line : (row + 1) * line] = silu_slope(affine) * group_gain
+
+    def pixel_taps(row):
+        for row_tap in range(3):
+            for time_tap in range(3):
+                at = (row_tap * 3 + time_tap) * piece
                 source = row - row_tap + 2
                 lane = source // half * 64
                 columns[row * FRAMES : (row + 1) * FRAMES, at : at + piece] = by_frame[
                     source % half, 2 - time_tap : 2 - time_tap + FRAMES, lane : lane + piece
                 ]
-    left = columns[...].astype(jnp.bfloat16)
+
+    for frame in range(FRAMES):
+        for row in range(half):
+            by_frame[row, frame : frame + 1, :] = arrived[slot_of[frame], row]
+    for row in range(1, own + 1):
+        pixel_taps(row)
+        state_terms(row)
+    left = columns[FRAMES : (own + 1) * FRAMES].astype(jnp.bfloat16)
+    first = jnp.zeros((1, channels), jnp.float32)
+    second = jnp.zeros((1, channels), jnp.float32)
     for w in range(0, wide, 2):
         both = jnp.dot(
             left,
@@ -557,23 +566,49 @@
             preferred_element_type=jnp.float32,
         )
         for side in range(2):
-            slope[pl.ds(w + side, (own + 2) * FRAMES, stride=wide), :] = both[
-                :, side * channels : (side + 1) * channels
-            ]
-
-    first = jnp.zeros((1, channels), jnp.float32)
-    second = jnp.zeros((1, channels), jnp.float32)
-    for row in range(own + 2):
-        part = pl.ds(row * line, line)
-        upstream = slope[part] * factor[part]
-        slope[part] = upstream
-        if 1 <= row <= own:
+            part = pl.ds(line + w + side, own * FRAMES, stride=wide)
+            upstream = both[:, side * channels : (side + 1) * channels] * factor[part]
+            slope[part] = upstream
             first = first + jnp.sum(upstream, axis=0, keepdims=True)
             second = second + jnp.sum(upstream * normed_ref[part], axis=0, keepdims=True)
     sums_two[me] = jnp.where(spot == 0, first, second)
-    two_copies = broadcast(sums_two, two_send, two_recv)
-
-    loads[3].wait()
+    broadcast(sums_two, 2)
+
+
+    @pl.when(me < n - 1)
+    def _():
+        to_right.wait_send()
+        to_left.wait_recv()
+
+    @pl.when(me > 0)
+    def _():
+        to_left.wait_send()
+        to_right.wait_recv()
+
+    for row in (0, own + 1):
+        pixel_taps(row)
+        state_terms(row)
+    left = jnp.concatenate(
+        [columns[0:FRAMES], columns[(own + 1) * FRAMES : (own + 2) * FRAMES]], axis=0
+    ).astype(jnp.bfloat16)
+    for w in range(0, wide, 2):
+        both = jnp.dot(
+            left,
+            band[:, w * channels : (w + 2) * channels],
+            preferred_element_type=jnp.float32,
+        )
+        for side in range(2):
+            for index, row in enumerate((0, own + 1)):
+                part = pl.ds(row * line + w + side, FRAMES, stride=wide)
+                slope[part] = (
+                    both[
+                        index * FRAMES : (index + 1) * FRAMES,
+                        side * channels : (side + 1) * channels,
+                    ]
+                    * factor[part]
+                )
+
+    load_inner.wait()
     for row_tap in range(3):
         for col_tap in range(3):
             part = pl.ds(col_tap * channels, channels)
@@ -584,15 +619,30 @@
             empty = jnp.zeros((channels, channels), jnp.bfloat16)
             turned[row_tap, 3, part, 0:channels] = empty
             turned[row_tap, 0, part, channels:] = empty
+    for row in range(own + 2):
+        part = pl.ds(row * line, line)
+        ready[part] = slope[part] * inverse
+
+    to_peers(sums_one, 0)
+    to_peers(arrived, 1)
+    to_peers(sums_two, 2)
+    from_peers(sums_two, 2)
+    total = over_devices(sums_two)
+    first, second = group_sums(total[0:1], total[1:2])
+    terms[0:2] = jnp.where(spot == 0, first, second) * (inverse / cell_total)
+
+
+def last_kernel(n, ready, normed_ref, terms, turned, out_any, windows, out, out_sem):
+    me = lax.axis_index("row")
+    own = out.shape[0]
+    wide = out.shape[3]
+    channels = out.shape[4]
+    line = FRAMES * wide
     windows[:, FRAMES // 2] = jnp.zeros((own + 2, 2, wide, 3 * channels), jnp.bfloat16)
-
-    for copy in two_copies:
-        copy.wait()
-    parts = group_sums(sums_two)
     position = lax.rem(lax.broadcasted_iota(jnp.int32, (line, channels), 0), wide)
     for row in range(own + 2):
         part = pl.ds(row * line, line)
-        state_grad = (slope[part] - parts[0:1] - normed_ref[part] * parts[1:2]) * inverse
+        state_grad = ready[part] - terms[0:1] - normed_ref[part] * terms[1:2]
         if row == 0:
             state_grad = jnp.where(me > 0, state_grad, 0.0)
         if row == own + 1:
@@ -603,28 +653,31 @@
             windows[row, 0 : FRAMES // 2, :, :, col_tap * channels : (col_tap + 1) * channels] = (
                 shifted.astype(jnp.bfloat16).reshape(FRAMES // 2, 2, wide, channels)
             )
-    rows = own * line // 2
-    taken = jnp.concatenate(
-        [
-            windows[
-                2 - row_tap : 2 - row_tap + own, ahead // 2 : ahead // 2 + FRAMES // 2, ahead % 2
-            ].reshape(rows, 3 * channels)
-            for row_tap in range(3)
-            for ahead in range(4)
-        ],
-        axis=1,
-    )
-    summed = jnp.dot(
-        taken,
-        turned[...].reshape(12 * 3 * channels, 2 * channels),
-        preferred_element_type=jnp.float32,
-    )
-    for side in range(2):
-        out[:, :, side] = (
-            summed[:, side * channels : (side + 1) * channels]
-            .reshape(own, FRAMES // 2, wide, channels)
-            .astype(jnp.bfloat16)
-        )
+    for row in range(own):
+        taken = jnp.concatenate(
+            [
+                windows[
+                    row + 2 - row_tap, ahead // 2 : ahead // 2 + FRAMES // 2, ahead % 2
+                ].reshape(line // 2, 3 * channels)
+                for row_tap in range(3)
+                for ahead in range(4)
+            ],
+            axis=1,
+        )
+        summed = jnp.dot(
+            taken,
+            turned[...].reshape(12 * 3 * channels, 2 * channels),
+            preferred_element_type=jnp.float32,
+        )
+        for side in range(2):
+            out[row, :, side] = (
+                summed[:, side * channels : (side + 1) * channels]
+                .reshape(FRAMES // 2, wide, channels)
+                .astype(jnp.bfloat16)
+            )
+        copy = pltpu.make_async_copy(out.at[row], out_any.at[row], out_sem)
+        copy.start()
+    pltpu.make_async_copy(out, out_any, out_sem).wait()
 
 
 def one_frame_each(
@@ -652,21 +705,23 @@
     f32, bf16 = jnp.float32, jnp.bfloat16
     vmem = pl.BlockSpec(memory_space=pltpu.VMEM)
     dma = pltpu.SemaphoreType.DMA
-    return pl.pallas_call(
+    passed = [
+        pltpu.VMEM((cells, channels), f32),
+        pltpu.VMEM((cells, channels), f32),
+        pltpu.VMEM((8, channels), f32),
+        pltpu.VMEM((3, 4, 3 * channels, 2 * channels), bf16),
+    ]
+    kept = pl.pallas_call(
         functools.partial(fused_kernel, n),
-        out_shape=jax.ShapeDtypeStruct((own, frame_count // 2, 2, wide, channels), bf16),
+        out_shape=passed,
         in_specs=[pl.BlockSpec(memory_space=pltpu.HBM)] * 14,
-        out_specs=vmem,
+        out_specs=[vmem] * 4,
         scratch_shapes=[
             pltpu.VMEM((3, strip, height), bf16),
             pltpu.SMEM(frame_owner.shape, jnp.int32),
             pltpu.SMEM(picks.shape, jnp.int32),
-            pltpu.VMEM((1, width), f32),
-            pltpu.VMEM((1, width), f32),
-            pltpu.VMEM((1, width), f32),
-            pltpu.VMEM((1, width), f32),
-            pltpu.VMEM((1, channels), f32),
-            pltpu.VMEM((1, channels), f32),
+            pltpu.VMEM((4, 1, width), f32),
+            pltpu.VMEM((2, 1, channels), f32),
             pltpu.VMEM(out_weight.shape, bf16),
             pltpu.VMEM((pix, width), bf16),
             pltpu.VMEM(head_weight.shape, bf16),
@@ -681,41 +736,51 @@
             pltpu.VMEM((depth, wide * channels), bf16),
             pltpu.VMEM((cells, channels), f32),
             pltpu.VMEM((cells, channels), f32),
-            pltpu.VMEM((cells, channels), f32),
-            pltpu.VMEM((3, 4, 3 * channels, 2 * channels), bf16),
-            pltpu.VMEM((own + 2, frame_count // 2 + 1, 2, wide, 3 * channels), bf16),
             pltpu.VMEM((n, 2, channels), f32),
             pltpu.VMEM((n, 2, channels), f32),
-            dma((4,)),
             dma((10,)),
             dma((2,)),
             dma((2,)),
-            dma((n,)),
-            dma((n,)),
-            dma((n,)),
-            dma((n,)),
-            dma((n,)),
-            dma((n,)),
+            dma((3,)),
+            dma((3,)),
         ],
         compiler_params=pltpu.CompilerParams(
-            collective_id=0, has_side_effects=True
+            collective_id=0, has_side_effects=True, vmem_limit_bytes=32 << 20
         ),
     )(
-        frames.transpose(0, 2, 1),
-        frame_owner,
-        picks,
-        patch_weight,
-        patch_bias[None],
-        norm_gain[None],
-        head_weight,
-        head_bias[None],
-        head_out[None],
-        hidden_state,
-        group_gain[None],
-        group_shift[None],
-        out_weight,
-        inner_weight,
-    ).reshape(hidden_state.shape)
+        *(
+            pltpu.with_memory_space_constraint(array, pltpu.HBM)
+            for array in (
+                frames.transpose(0, 2, 1),
+                frame_owner,
+                picks,
+                patch_weight,
+                patch_bias[None],
+                norm_gain[None],
+                head_weight,
+                head_bias[None],
+                head_out[None],
+                hidden_state,
+                group_gain[None],
+                group_shift[None],
+                out_weight,
+                inner_weight,
+            )
+        )
+    )
+    out_shape = (own, frame_count // 2, 2, wide, channels)
+    return pl.pallas_call(
+        functools.partial(last_kernel, n),
+        out_shape=jax.ShapeDtypeStruct(out_shape, bf16),
+        in_specs=[vmem] * 4,
+        out_specs=pl.BlockSpec(memory_space=pltpu.HBM),
+        scratch_shapes=[
+            pltpu.VMEM((own + 2, frame_count // 2 + 1, 2, wide, 3 * channels), bf16),
+            pltpu.VMEM(out_shape, bf16),
+            dma,
+        ],
+        compiler_params=pltpu.CompilerParams(vmem_limit_bytes=32 << 20),
+    )(*kept).reshape(hidden_state.shape)
 
 
 def solution(mesh):

time: 21.2 us -> 17.8 us (0.84)
  Pallas kernels: 19.4 us -> 17.6 us
  local copies, waits for them, and re-layouts: 1.62 us -> 0 us
    pallas_call x1 -> x2, Pallas kernels: 19.4 us -> 17.6 us  [the longest x1 15.6 us: one_frame_each(): pl.pallas_call(functools.partial(fused_kernel, n), out_shape=passed, in_s...]
    unnamed x1 -> x0, local copies, waits for them, and re-layouts: 1.62 us -> none
where the time goes in v2:
time: 17.8 us; the launch traced here: 17.6 us
  Pallas kernels  17.6 us (99%)
    pallas_call x1, Pallas kernels, one_frame_each(): pl.pallas_call(functools.partial(fused_kernel, n), out_shape=passed, in_s...  15.6 us
    pallas_call x1, Pallas kernels, one_frame_each(): pl.pallas_call(functools.partial(last_kernel, n), out_shape=jax.ShapeDtyp...  1.97 us

profile of v2, /device:TPU:0, one launch (start us, length us, event | category | flops | bytes accessed | tf_op | source)
XLA Modules:
  0.0 17.6 jit_solution(7967474756597699031)
XLA Ops:
  0.0 15.6 %shard_map.136 = (f32[1280,128]{1,0:T(8,128)S(1)}, f32[1280,128]{1,0:T(8,128)S(1)}, f32[8,128]{1,0:T(8,128)S(1)}, bf16[3,4,384,256]{3,2,1,0:T(8,128)(2,1)S(1)}) custom-call(bf16[3,16,48]{2,1,0:T(8,128)(2,1)} %bitcast.8, s32[16]{0:T(128)} %owner_any.1, s32[8]{0:T(128)} %picks_any.1, bf16[768,1024]{1,0:T(8,128)(2,1)} %patch_any.1, f32[1,1024]{1,0:T(1,128)} %bitcast.9, ...), custom_call_target="tpu_custom_call" | custom-call | tf_op jit(solution)/shard_map/pallas_call | solution.py:714
  15.6 2.0 %shard_map.137 = bf16[3,8,2,16,128]{4,3,2,1,0:T(8,128)(2,1)} custom-call(f32[1280,128]{1,0:T(8,128)S(1)} %get-tuple-element.9.ready, f32[1280,128]{1,0:T(8,128)S(1)} %get-tuple-element.10.normed_ref, f32[8,128]{1,0:T(8,128)S(1)} %get-tuple-element.11.terms, bf16[3,4,384,256]{3,2,1,0:T(8,128)(2,1)S(1)} %get-tuple-element.12.turned), custom_call_target="tpu_custom_call" | custom-call | tf_op jit(solution)/shard_map/pallas_call | solution.py:772

commit v3 on v2

--- a/solution.py
+++ b/solution.py
@@ -239,9 +239,12 @@
     arrived,
     by_frame,
     columns,
+    taps,
     band,
     slope,
+    cells,
     factor,
+    normed_cells,
     sums_one,
     sums_two,
     local_sem,
@@ -257,9 +260,12 @@
     wide = hidden.shape[2]
     channels = hidden.shape[3]
     line = FRAMES * wide
+    pitch = wide + 1
     per_group = channels // GROUPS
     cell_total = own * n * FRAMES * wide * per_group
-    piece = 3 * strip
+    window = wide // 2 + 1
+    piece = 3 * window
+    slot_lanes = 64
     half = arrived.shape[1]
 
     def peer(offset):
@@ -279,8 +285,24 @@
 
     load_frames = pltpu.make_async_copy(frames_any, frames, local_sem.at[0])
     load_hidden = pltpu.make_async_copy(hidden_any, hidden.at[pl.ds(1, own)], local_sem.at[1])
-    load_patch = pltpu.make_async_copy(patch_any, patch_w, local_sem.at[2])
-    load_head = pltpu.make_async_copy(head_any, head_w, local_sem.at[3])
+    pix, width = patch_w.shape
+    third, part_rows = pix // 3, width // 2
+    load_patch = [
+        pltpu.make_async_copy(
+            patch_any.at[pl.ds(part * third, third)],
+            patch_w.at[pl.ds(part * third, third)],
+            local_sem.at[10 + part],
+        )
+        for part in range(3)
+    ]
+    load_head = [
+        pltpu.make_async_copy(
+            head_any.at[pl.ds(part * part_rows, part_rows)],
+            head_w.at[pl.ds(part * part_rows, part_rows)],
+            local_sem.at[13 + part],
+        )
+        for part in range(2)
+    ]
     load_inner = pltpu.make_async_copy(inner_any, inner_w, local_sem.at[4])
     load_out = pltpu.make_async_copy(out_weight_any, out_weight, local_sem.at[5])
     load_owner = pltpu.make_async_copy(owner_any, owner, local_sem.at[6])
@@ -295,13 +317,17 @@
     ]
     load_frames.start()
     load_hidden.start()
-    load_patch.start()
-    for load in load_wide + load_group:
+    for load in load_patch:
+        load.start()
+    for load in load_wide:
+        load.start()
+    for load in load_head:
         load.start()
     load_owner.start()
     load_picks.start()
+    for load in load_group:
+        load.start()
     load_out.start()
-    load_head.start()
     load_inner.start()
 
     group_row = lax.broadcasted_iota(jnp.int32, (channels, channels), 0) // per_group
@@ -327,14 +353,16 @@
             jnp.sum(summed[4:8], axis=0, keepdims=True),
         )
 
-    def over_devices(buffer):
-        blocks = [buffer[slot] for slot in range(n)]
+    def tree_sum(blocks):
         while len(blocks) > 1:
             blocks = [
                 blocks[at] + blocks[at + 1] if at + 1 < len(blocks) else blocks[at]
                 for at in range(0, len(blocks), 2)
             ]
         return blocks[0]
+
+    def over_devices(buffer):
+        return tree_sum([buffer[slot] for slot in range(n)])
 
     load_frames.wait()
     for colour in range(3):
@@ -359,31 +387,32 @@
     sums_one[me] = jnp.where(spot == 0, first, second)
 
     pltpu.make_async_copy(wide_rows, wide_rows, local_sem.at[8]).wait()
-    pltpu.make_async_copy(group_rows, group_rows, local_sem.at[9]).wait()
-    load_owner.wait()
-    load_picks.wait()
-    load_out.wait()
-    load_patch.wait()
-    embedded = (
-        jnp.dot(
-            tokens[...].astype(jnp.bfloat16), patch_w[...], preferred_element_type=jnp.float32
-        )
-        + wide_rows[0]
-    )
+    embedded = wide_rows[0]
+    for part in range(3):
+        load_patch[part].wait()
+        embedded = embedded + jnp.dot(
+            tokens[:, part * third : (part + 1) * third].astype(jnp.bfloat16),
+            patch_w[part * third : (part + 1) * third],
+            preferred_element_type=jnp.float32,
+        )
     centred = embedded - jnp.mean(embedded, axis=1, keepdims=True)
     inv_spread = lax.rsqrt(jnp.mean(centred * centred, axis=1, keepdims=True) + eps_norm)
     normed = centred * inv_spread
     gain = wide_rows[1]
     pooled = jnp.sum((normed * gain)[0:patch_rows], axis=0, keepdims=True) / patch_rows
-    load_head.wait()
-    before = (
-        jnp.sum(
-            jnp.dot(split_rows(pooled), head_w[...], preferred_element_type=jnp.float32),
+    split_pool = split_rows(pooled)
+    before = wide_rows[2]
+    for part in range(2):
+        load_head[part].wait()
+        before = before + jnp.sum(
+            jnp.dot(
+                split_pool[:, part * part_rows : (part + 1) * part_rows],
+                head_w[part * part_rows : (part + 1) * part_rows],
+                preferred_element_type=jnp.float32,
+            ),
             axis=0,
             keepdims=True,
         )
-        + wide_rows[2]
-    )
     pulled = jnp.sum(
         lax.dot_general(
             split_rows(wide_rows[3] * silu_slope(before)),
@@ -394,6 +423,8 @@
         axis=0,
         keepdims=True,
     )
+    load_owner.wait()
+    load_picks.wait()
     mine = owner[me]
     picked = jnp.float32(0.0)
     for pick in range(picks.shape[0]):
@@ -412,18 +443,21 @@
     )
     patch_grad = patch_grad.astype(jnp.bfloat16).astype(jnp.float32)
     for line_in in range(PATCH):
+        lines = [
+            patch_grad[:, (colour * PATCH + line_in) * PATCH : (colour * PATCH + line_in + 1) * PATCH]
+            for colour in range(3)
+        ]
         joined = jnp.concatenate(
-            [
-                patch_grad[:, (colour * PATCH + line_in) * PATCH : (colour * PATCH + line_in + 1) * PATCH]
-                for colour in range(3)
-            ],
+            [line_of[:, 0:window] for line_of in lines]
+            + [jnp.zeros((lines[0].shape[0], slot_lanes - 2 * piece), jnp.float32)]
+            + [line_of[:, wide - window : wide] for line_of in lines],
             axis=1,
         )
         for patch_row in range(patch_rows):
             at = 2 + patch_row * PATCH + line_in
-            sent[at, :, 0:piece] = joined[patch_row : patch_row + 1]
+            sent[at, :, 0:slot_lanes] = joined[patch_row : patch_row + 1]
             if at >= half:
-                sent[at - half, :, 64 : 64 + piece] = joined[patch_row : patch_row + 1]
+                sent[at - half, :, slot_lanes : 2 * slot_lanes] = joined[patch_row : patch_row + 1]
 
     pl.semaphore_wait(barrier, n - 1)
 
@@ -492,29 +526,35 @@
 
     arrived[me] = sent[pl.ds(me * own, half)]
 
-    column = lax.broadcasted_iota(jnp.int32, (wide, channels), 0)
-    for row_tap in range(3):
-        for time_tap in range(3):
-            taps = [out_weight[time_tap, row_tap, col_tap].astype(jnp.float32) for col_tap in range(3)]
-            for colour in range(3):
-                at = ((row_tap * 3 + time_tap) * 3 + colour) * wide
-                spread = [
-                    jnp.broadcast_to(tap[colour : colour + 1], (wide, channels)) for tap in taps
-                ]
-                for w in range(wide):
-                    block = jnp.where(
-                        column == w + 1,
-                        spread[0],
-                        jnp.where(
-                            column == w, spread[1], jnp.where(column == w - 1, spread[2], 0.0)
-                        ),
-                    )
-                    band[at : at + wide, w * channels : (w + 1) * channels] = block.astype(
-                        jnp.bfloat16
-                    )
+    load_out.wait()
+    taps[...] = jnp.zeros_like(taps)
+    for time_tap in range(3):
+        for row_tap in range(3):
+            for col_tap in range(3):
+                at = ((time_tap * 3 + row_tap) * 3 + col_tap) * 3
+                taps[at : at + 3] = out_weight[time_tap, row_tap, col_tap].astype(jnp.float32)
+    flat_taps = taps[...].astype(jnp.bfloat16)
     depth = band.shape[0]
-    if depth > 27 * wide:
-        band[27 * wide :, :] = jnp.zeros((depth - 27 * wide, wide * channels), jnp.bfloat16)
+    entry = lax.broadcasted_iota(jnp.int32, (depth, channels), 0)
+    tap_lane = lax.broadcasted_iota(jnp.int32, (depth, channels), 1)
+    tap_of = entry // piece
+    column = lax.rem(entry, window)
+    first_lane = (
+        (lax.rem(tap_of, 3) * 3 + tap_of // 3) * 9 + lax.rem(entry, piece) // window - 3 * column
+    )
+    for output in range(window):
+        col_tap = output + 1 - column
+        chosen = (
+            (tap_lane == first_lane + 3 * (output + 1))
+            & (col_tap >= 0)
+            & (col_tap < 3)
+            & (entry < 9 * piece)
+        )
+        band[:, output * channels : (output + 1) * channels] = jnp.dot(
+            chosen.astype(jnp.float32).astype(jnp.bfloat16),
+            flat_taps,
+            preferred_element_type=jnp.float32,
+        ).astype(jnp.bfloat16)
     columns[...] = jnp.zeros_like(columns)
     by_frame[...] = jnp.zeros_like(by_frame)
 
@@ -525,88 +565,14 @@
             found = jnp.where(owner[slot] == frame, jnp.int32(slot), found)
         slot_of.append(found)
 
-    from_peers(sums_one, 0)
-    from_peers(arrived, 1)
-    means = over_devices(sums_one) / cell_total
-    group_mean = means[0:1]
-    inverse = lax.rsqrt(means[1:2] - group_mean * group_mean + eps_norm)
-    group_gain = group_rows[0]
-    group_shift = group_rows[1]
-
-    def state_terms(row):
-        state = hidden[row].reshape(line, channels).astype(jnp.float32)
-        normed_state = (state - group_mean) * inverse
-        normed_ref[row * line : (row + 1) * line] = normed_state
-        affine = normed_state * group_gain + group_shift
-        factor[row * line : (row + 1) * line] = silu_slope(affine) * group_gain
-
-    def pixel_taps(row):
-        for row_tap in range(3):
-            for time_tap in range(3):
-                at = (row_tap * 3 + time_tap) * piece
-                source = row - row_tap + 2
-                lane = source // half * 64
-                columns[row * FRAMES : (row + 1) * FRAMES, at : at + piece] = by_frame[
-                    source % half, 2 - time_tap : 2 - time_tap + FRAMES, lane : lane + piece
-                ]
-
-    for frame in range(FRAMES):
-        for row in range(half):
-            by_frame[row, frame : frame + 1, :] = arrived[slot_of[frame], row]
+
+    def spread_cells(row):
+        for frame in range(FRAMES):
+            at = (row * FRAMES + frame) * pitch
+            cells[at : at + wide] = hidden[row, frame].astype(jnp.float32)
+
     for row in range(1, own + 1):
-        pixel_taps(row)
-        state_terms(row)
-    left = columns[FRAMES : (own + 1) * FRAMES].astype(jnp.bfloat16)
-    first = jnp.zeros((1, channels), jnp.float32)
-    second = jnp.zeros((1, channels), jnp.float32)
-    for w in range(0, wide, 2):
-        both = jnp.dot(
-            left,
-            band[:, w * channels : (w + 2) * channels],
-            preferred_element_type=jnp.float32,
-        )
-        for side in range(2):
-            part = pl.ds(line + w + side, own * FRAMES, stride=wide)
-            upstream = both[:, side * channels : (side + 1) * channels] * factor[part]
-            slope[part] = upstream
-            first = first + jnp.sum(upstream, axis=0, keepdims=True)
-            second = second + jnp.sum(upstream * normed_ref[part], axis=0, keepdims=True)
-    sums_two[me] = jnp.where(spot == 0, first, second)
-    broadcast(sums_two, 2)
-
-
-    @pl.when(me < n - 1)
-    def _():
-        to_right.wait_send()
-        to_left.wait_recv()
-
-    @pl.when(me > 0)
-    def _():
-        to_left.wait_send()
-        to_right.wait_recv()
-
-    for row in (0, own + 1):
-        pixel_taps(row)
-        state_terms(row)
-    left = jnp.concatenate(
-        [columns[0:FRAMES], columns[(own + 1) * FRAMES : (own + 2) * FRAMES]], axis=0
-    ).astype(jnp.bfloat16)
-    for w in range(0, wide, 2):
-        both = jnp.dot(
-            left,
-            band[:, w * channels : (w + 2) * channels],
-            preferred_element_type=jnp.float32,
-        )
-        for side in range(2):
-            for index, row in enumerate((0, own + 1)):
-                part = pl.ds(row * line + w + side, FRAMES, stride=wide)
-                slope[part] = (
-                    both[
-                        index * FRAMES : (index + 1) * FRAMES,
-                        side * channels : (side + 1) * channels,
-                    ]
-                    * factor[part]
-                )
+        spread_cells(row)
 
     load_inner.wait()
     for row_tap in range(3):
@@ -619,9 +585,106 @@
             empty = jnp.zeros((channels, channels), jnp.bfloat16)
             turned[row_tap, 3, part, 0:channels] = empty
             turned[row_tap, 0, part, channels:] = empty
-    for row in range(own + 2):
-        part = pl.ds(row * line, line)
-        ready[part] = slope[part] * inverse
+    pltpu.make_async_copy(group_rows, group_rows, local_sem.at[9]).wait()
+    from_peers(sums_one, 0)
+    from_peers(arrived, 1)
+    means = over_devices(sums_one) / cell_total
+    group_mean = means[0:1]
+    inverse = lax.rsqrt(means[1:2] - group_mean * group_mean + eps_norm)
+    group_gain = group_rows[0]
+    group_shift = group_rows[1]
+
+    def pixel_taps(row, block):
+        for row_tap in range(3):
+            for time_tap in range(3):
+                at = (row_tap * 3 + time_tap) * piece
+                source = row - row_tap + 2
+                for side in range(2):
+                    lane = source // half * slot_lanes + side * (slot_lanes - piece)
+                    columns[block[side] : block[side] + FRAMES, at : at + piece] = by_frame[
+                        source % half, 2 - time_tap : 2 - time_tap + FRAMES, lane : lane + piece
+                    ]
+
+    def state_terms(part):
+        normed_state = (cells[part] - group_mean) * inverse
+        return normed_state, silu_slope(normed_state * group_gain + group_shift) * group_gain
+
+    own_cells = own * FRAMES
+    for w in range(wide):
+        normed_state, slope_factor = state_terms(
+            pl.ds(FRAMES * pitch + w, own_cells, stride=pitch)
+        )
+        normed_cells[w] = normed_state
+        factor[w] = slope_factor
+    for frame in range(FRAMES):
+        for row in range(half):
+            by_frame[row, frame : frame + 1, :] = arrived[slot_of[frame], row]
+    for row in range(1, own + 1):
+        pixel_taps(row, ((row - 1) * FRAMES, own_cells + (row - 1) * FRAMES))
+    left = columns[0 : 2 * own_cells].astype(jnp.bfloat16)
+    firsts, seconds = [], []
+    for output in range(0, window, 2):
+        lanes = pl.ds(output * channels, min(2, window - output) * channels)
+        several = jnp.dot(left, band[:, lanes], preferred_element_type=jnp.float32)
+        for index in range(several.shape[1] // channels):
+            for side in range(2):
+                w = output + index + side * (wide - window)
+                if side == 0 and output + index == window - 1 or side == 1 and output + index == 0:
+                    continue
+                upstream = (
+                    several[
+                        side * own_cells : (side + 1) * own_cells,
+                        index * channels : (index + 1) * channels,
+                    ]
+                    * factor[w]
+                )
+                slope[pl.ds(FRAMES * pitch + w, own_cells, stride=pitch)] = upstream
+                firsts.append(jnp.sum(upstream.reshape(-1, 8, channels), axis=0))
+                seconds.append(
+                    jnp.sum((upstream * normed_cells[w]).reshape(-1, 8, channels), axis=0)
+                )
+    first = tree_sum(firsts)
+    second = tree_sum(seconds)
+    first = jnp.sum(first, axis=0, keepdims=True)
+    second = jnp.sum(second, axis=0, keepdims=True)
+    sums_two[me] = jnp.where(spot == 0, first, second)
+    broadcast(sums_two, 2)
+
+
+    @pl.when(me < n - 1)
+    def _():
+        to_right.wait_send()
+        to_left.wait_recv()
+
+    @pl.when(me > 0)
+    def _():
+        to_left.wait_send()
+        to_right.wait_recv()
+
+    for index, row in enumerate((0, own + 1)):
+        pixel_taps(row, (2 * own_cells + index * FRAMES, 2 * own_cells + (2 + index) * FRAMES))
+        spread_cells(row)
+    left = columns[2 * own_cells :].astype(jnp.bfloat16)
+    for output in range(window):
+        several = jnp.dot(
+            left,
+            band[:, output * channels : (output + 1) * channels],
+            preferred_element_type=jnp.float32,
+        )
+        for side in range(2):
+            if side == 0 and output == window - 1 or side == 1 and output == 0:
+                continue
+            for index, row in enumerate((0, own + 1)):
+                part = pl.ds(
+                    row * FRAMES * pitch + output + side * (wide - window), FRAMES, stride=pitch
+                )
+                at = (2 * side + index) * FRAMES
+                slope[part] = several[at : at + FRAMES] * state_terms(part)[1]
+    for cell in range((own + 2) * FRAMES):
+        part = pl.ds(cell * wide, wide)
+        ready[part] = slope[cell * pitch : cell * pitch + wide] * inverse
+        state = hidden[cell // FRAMES, cell % FRAMES].astype(jnp.float32)
+        normed_ref[part] = (state - group_mean) * inverse
 
     to_peers(sums_one, 0)
     to_peers(arrived, 1)
@@ -700,7 +763,8 @@
     own, frame_count, wide, channels = hidden_state.shape
     height, strip = frames.shape[1:]
     pix, width = patch_weight.shape
-    depth = -(-27 * wide // 128) * 128
+    window = wide // 2 + 1
+    depth = -(-27 * window // 128) * 128
     cells = (own + 2) * frame_count * wide
     f32, bf16 = jnp.float32, jnp.bfloat16
     vmem = pl.BlockSpec(memory_space=pltpu.VMEM)
@@ -732,13 +796,16 @@
             pltpu.VMEM((height + 4, 1, 128), f32),
             pltpu.VMEM((n, (own + 5) // 2, 1, 128), f32),
             pltpu.VMEM(((own + 5) // 2, frame_count + 8, 128), f32),
-            pltpu.VMEM(((own + 2) * frame_count, depth), f32),
-            pltpu.VMEM((depth, wide * channels), bf16),
-            pltpu.VMEM((cells, channels), f32),
-            pltpu.VMEM((cells, channels), f32),
+            pltpu.VMEM((2 * (own + 2) * frame_count, depth), f32),
+            pltpu.VMEM((128, channels), f32),
+            pltpu.VMEM((depth, window * channels), bf16),
+            pltpu.VMEM(((own + 2) * frame_count * (wide + 1), channels), f32),
+            pltpu.VMEM(((own + 2) * frame_count * (wide + 1), channels), f32),
+            pltpu.VMEM((wide, own * frame_count, channels), f32),
+            pltpu.VMEM((wide, own * frame_count, channels), f32),
             pltpu.VMEM((n, 2, channels), f32),
             pltpu.VMEM((n, 2, channels), f32),
-            dma((10,)),
+            dma((15,)),
             dma((2,)),
             dma((2,)),
             dma((3,)),

time: 17.8 us -> 17.3 us (0.972)
  Pallas kernels: 17.6 us -> 17 us
    pallas_call x1, Pallas kernels: 15.6 us -> 15.1 us  [one_frame_each(): pl.pallas_call(functools.partial(fused_kernel, n), out_shape=passed, in_s...]
where the time goes in v3:
time: 17.3 us; the launch traced here: 17 us
  Pallas kernels  17 us (98%)
    pallas_call x1, Pallas kernels, one_frame_each(): pl.pallas_call(functools.partial(fused_kernel, n), out_shape=passed, in_s...  15.1 us
    pallas_call x1, Pallas kernels, one_frame_each(): pl.pallas_call(functools.partial(last_kernel, n), out_shape=jax.ShapeDtyp...  1.97 us

profile of v3, /device:TPU:0, one launch (start us, length us, event | category | flops | bytes accessed | tf_op | source)
XLA Modules:
  0.0 17.0 jit_solution(14869380657540889145)
XLA Ops:
  0.0 15.1 %shard_map.136 = (f32[1280,128]{1,0:T(8,128)S(1)}, f32[1280,128]{1,0:T(8,128)S(1)}, f32[8,128]{1,0:T(8,128)S(1)}, bf16[3,4,384,256]{3,2,1,0:T(8,128)(2,1)S(1)}) custom-call(bf16[3,16,48]{2,1,0:T(8,128)(2,1)} %bitcast.8, s32[16]{0:T(128)} %owner_any.1, s32[8]{0:T(128)} %picks_any.1, bf16[768,1024]{1,0:T(8,128)(2,1)} %patch_any.1, f32[1,1024]{1,0:T(1,128)} %bitcast.9, ...), custom_call_target="tpu_custom_call" | custom-call | tf_op jit(solution)/shard_map/pallas_call | solution.py:778
  15.1 2.0 %shard_map.137 = bf16[3,8,2,16,128]{4,3,2,1,0:T(8,128)(2,1)} custom-call(f32[1280,128]{1,0:T(8,128)S(1)} %get-tuple-element.9.ready, f32[1280,128]{1,0:T(8,128)S(1)} %get-tuple-element.10.normed_ref, f32[8,128]{1,0:T(8,128)S(1)} %get-tuple-element.11.terms, bf16[3,4,384,256]{3,2,1,0:T(8,128)(2,1)S(1)} %get-tuple-element.12.turned), custom_call_target="tpu_custom_call" | custom-call | tf_op jit(solution)/shard_map/pallas_call | solution.py:839

commit v4 on v3

--- a/solution.py
+++ b/solution.py
@@ -244,11 +244,10 @@
     slope,
     cells,
     factor,
-    normed_cells,
+    centred_cells,
     sums_one,
     sums_two,
     local_sem,
-    halo_send,
     halo_recv,
     send_sem,
     recv_sem,
@@ -291,7 +290,7 @@
         pltpu.make_async_copy(
             patch_any.at[pl.ds(part * third, third)],
             patch_w.at[pl.ds(part * third, third)],
-            local_sem.at[10 + part],
+            local_sem.at[7 + part],
         )
         for part in range(3)
     ]
@@ -299,20 +298,20 @@
         pltpu.make_async_copy(
             head_any.at[pl.ds(part * part_rows, part_rows)],
             head_w.at[pl.ds(part * part_rows, part_rows)],
-            local_sem.at[13 + part],
+            local_sem.at[10 + part],
         )
         for part in range(2)
     ]
     load_inner = pltpu.make_async_copy(inner_any, inner_w, local_sem.at[4])
     load_out = pltpu.make_async_copy(out_weight_any, out_weight, local_sem.at[5])
-    load_owner = pltpu.make_async_copy(owner_any, owner, local_sem.at[6])
-    load_picks = pltpu.make_async_copy(picks_any, picks, local_sem.at[7])
+    load_owner = pltpu.make_async_copy(owner_any, owner, local_sem.at[5])
+    load_picks = pltpu.make_async_copy(picks_any, picks, local_sem.at[5])
     load_wide = [
-        pltpu.make_async_copy(source, wide_rows.at[index], local_sem.at[8])
+        pltpu.make_async_copy(source, wide_rows.at[index], local_sem.at[6])
         for index, source in enumerate((patch_bias_any, norm_gain_any, head_bias_any, head_out_any))
     ]
     load_group = [
-        pltpu.make_async_copy(source, group_rows.at[index], local_sem.at[9])
+        pltpu.make_async_copy(source, group_rows.at[index], local_sem.at[5])
         for index, source in enumerate((group_gain_any, group_shift_any))
     ]
     load_frames.start()
@@ -386,7 +385,7 @@
     first, second = group_sums(first, second)
     sums_one[me] = jnp.where(spot == 0, first, second)
 
-    pltpu.make_async_copy(wide_rows, wide_rows, local_sem.at[8]).wait()
+    pltpu.make_async_copy(wide_rows, wide_rows, local_sem.at[6]).wait()
     embedded = wide_rows[0]
     for part in range(3):
         load_patch[part].wait()
@@ -425,6 +424,8 @@
     )
     load_owner.wait()
     load_picks.wait()
+    pltpu.make_async_copy(group_rows, group_rows, local_sem.at[5]).wait()
+    load_out.wait()
     mine = owner[me]
     picked = jnp.float32(0.0)
     for pick in range(picks.shape[0]):
@@ -435,11 +436,20 @@
         - jnp.mean(scaled, axis=1, keepdims=True)
         - normed * jnp.mean(scaled * normed, axis=1, keepdims=True)
     )
-    patch_grad = lax.dot_general(
-        token_grad.astype(jnp.bfloat16),
-        patch_w[...],
-        (((1,), (1,)), ((), ())),
-        preferred_element_type=jnp.float32,
+    token_grad = token_grad.astype(jnp.bfloat16)
+    sixth = pix // 6
+    cuts = (0, 3, 6)
+    patch_grad = jnp.concatenate(
+        [
+            lax.dot_general(
+                token_grad,
+                patch_w[low * sixth : high * sixth],
+                (((1,), (1,)), ((), ())),
+                preferred_element_type=jnp.float32,
+            )
+            for low, high in zip(cuts[:-1], cuts[1:])
+        ],
+        axis=1,
     )
     patch_grad = patch_grad.astype(jnp.bfloat16).astype(jnp.float32)
     for line_in in range(PATCH):
@@ -461,40 +471,39 @@
 
     pl.semaphore_wait(barrier, n - 1)
 
-    def broadcast(buffer, kind):
-        for offset in farthest_first:
-            pltpu.make_async_remote_copy(
-                src_ref=buffer.at[me],
-                dst_ref=buffer.at[me],
-                send_sem=send_sem.at[kind],
-                recv_sem=recv_sem.at[kind],
-                device_id={"row": peer(offset)},
-                device_id_type=MESH,
-            ).start()
+    def send_sums(buffer, kind, offset):
+        pltpu.make_async_remote_copy(
+            src_ref=buffer.at[me],
+            dst_ref=buffer.at[me],
+            send_sem=send_sem,
+            recv_sem=recv_sem.at[kind],
+            device_id={"row": peer(offset)},
+            device_id_type=MESH,
+        ).start()
 
     def from_peers(buffer, kind):
         others = buffer.at[pl.ds(0, n - 1)]
         pltpu.make_async_copy(others, others, recv_sem.at[kind]).wait()
 
-    def to_peers(buffer, kind):
+    def to_peers(buffer):
         others = buffer.at[pl.ds(0, n - 1)]
-        pltpu.make_async_copy(others, others, send_sem.at[kind]).wait()
+        pltpu.make_async_copy(others, others, send_sem).wait()
 
     for offset in farthest_first:
         target = peer(offset)
         pltpu.make_async_remote_copy(
             src_ref=sent.at[pl.ds(target * own, half)],
             dst_ref=arrived.at[me],
-            send_sem=send_sem.at[1],
+            send_sem=send_sem,
             recv_sem=recv_sem.at[1],
             device_id={"row": target},
             device_id_type=MESH,
         ).start()
-    broadcast(sums_one, 0)
+        send_sums(sums_one, 0, offset)
     to_right = pltpu.make_async_remote_copy(
         src_ref=hidden_any.at[pl.ds(own - 1, 1)],
         dst_ref=hidden.at[pl.ds(0, 1)],
-        send_sem=halo_send.at[0],
+        send_sem=send_sem,
         recv_sem=halo_recv.at[0],
         device_id={"row": lax.rem(me + 1, n)},
         device_id_type=MESH,
@@ -502,7 +511,7 @@
     to_left = pltpu.make_async_remote_copy(
         src_ref=hidden_any.at[pl.ds(0, 1)],
         dst_ref=hidden.at[pl.ds(own + 1, 1)],
-        send_sem=halo_send.at[1],
+        send_sem=send_sem,
         recv_sem=halo_recv.at[1],
         device_id={"row": lax.rem(me + n - 1, n)},
         device_id_type=MESH,
@@ -526,7 +535,6 @@
 
     arrived[me] = sent[pl.ds(me * own, half)]
 
-    load_out.wait()
     taps[...] = jnp.zeros_like(taps)
     for time_tap in range(3):
         for row_tap in range(3):
@@ -585,15 +593,13 @@
             empty = jnp.zeros((channels, channels), jnp.bfloat16)
             turned[row_tap, 3, part, 0:channels] = empty
             turned[row_tap, 0, part, channels:] = empty
-    pltpu.make_async_copy(group_rows, group_rows, local_sem.at[9]).wait()
     from_peers(sums_one, 0)
-    from_peers(arrived, 1)
     means = over_devices(sums_one) / cell_total
     group_mean = means[0:1]
     inverse = lax.rsqrt(means[1:2] - group_mean * group_mean + eps_norm)
     group_gain = group_rows[0]
     group_shift = group_rows[1]
-
+    from_peers(arrived, 1)
     def pixel_taps(row, block):
         for row_tap in range(3):
             for time_tap in range(3):
@@ -605,17 +611,16 @@
                         source % half, 2 - time_tap : 2 - time_tap + FRAMES, lane : lane + piece
                     ]
 
+    spread = inverse * group_gain
+
     def state_terms(part):
-        normed_state = (cells[part] - group_mean) * inverse
-        return normed_state, silu_slope(normed_state * group_gain + group_shift) * group_gain
+        centred = cells[part] - group_mean
+        return centred, silu_slope(centred * spread + group_shift)
 
     own_cells = own * FRAMES
     for w in range(wide):
-        normed_state, slope_factor = state_terms(
-            pl.ds(FRAMES * pitch + w, own_cells, stride=pitch)
-        )
-        normed_cells[w] = normed_state
-        factor[w] = slope_factor
+        part = pl.ds(FRAMES * pitch + w, own_cells, stride=pitch)
+        centred_cells[w], factor[w] = state_terms(part)
     for frame in range(FRAMES):
         for row in range(half):
             by_frame[row, frame : frame + 1, :] = arrived[slot_of[frame], row]
@@ -641,24 +646,23 @@
                 slope[pl.ds(FRAMES * pitch + w, own_cells, stride=pitch)] = upstream
                 firsts.append(jnp.sum(upstream.reshape(-1, 8, channels), axis=0))
                 seconds.append(
-                    jnp.sum((upstream * normed_cells[w]).reshape(-1, 8, channels), axis=0)
+                    jnp.sum((upstream * centred_cells[w]).reshape(-1, 8, channels), axis=0)
                 )
     first = tree_sum(firsts)
     second = tree_sum(seconds)
-    first = jnp.sum(first, axis=0, keepdims=True)
-    second = jnp.sum(second, axis=0, keepdims=True)
+    first = jnp.sum(first, axis=0, keepdims=True) * group_gain
+    second = jnp.sum(second, axis=0, keepdims=True) * spread
     sums_two[me] = jnp.where(spot == 0, first, second)
-    broadcast(sums_two, 2)
+    for offset in farthest_first:
+        send_sums(sums_two, 2, offset)
 
 
     @pl.when(me < n - 1)
     def _():
-        to_right.wait_send()
         to_left.wait_recv()
 
     @pl.when(me > 0)
     def _():
-        to_left.wait_send()
         to_right.wait_recv()
 
     for index, row in enumerate((0, own + 1)):
@@ -682,17 +686,34 @@
                 slope[part] = several[at : at + FRAMES] * state_terms(part)[1]
     for cell in range((own + 2) * FRAMES):
         part = pl.ds(cell * wide, wide)
-        ready[part] = slope[cell * pitch : cell * pitch + wide] * inverse
+        ready[part] = slope[cell * pitch : cell * pitch + wide] * spread
         state = hidden[cell // FRAMES, cell % FRAMES].astype(jnp.float32)
         normed_ref[part] = (state - group_mean) * inverse
 
-    to_peers(sums_one, 0)
-    to_peers(arrived, 1)
-    to_peers(sums_two, 2)
+    to_peers(sums_one)
+    to_peers(arrived)
+    to_peers(sums_two)
+
+    @pl.when(me < n - 1)
+    def _():
+        to_right.wait_send()
+
+    @pl.when(me > 0)
+    def _():
+        to_left.wait_send()
+
     from_peers(sums_two, 2)
     total = over_devices(sums_two)
-    first, second = group_sums(total[0:1], total[1:2])
-    terms[0:2] = jnp.where(spot == 0, first, second) * (inverse / cell_total)
+    lane = lax.broadcasted_iota(jnp.int32, total.shape, 1)
+    step = 1
+    while step < per_group:
+        total = total + jnp.where(
+            lax.rem(lane // step, 2) == 0,
+            pltpu.roll(total, channels - step, 1),
+            pltpu.roll(total, step, 1),
+        )
+        step *= 2
+    terms[0:2] = total * (inverse / cell_total)
 
 
 def last_kernel(n, ready, normed_ref, terms, turned, out_any, windows, out, out_sem):
@@ -805,10 +826,9 @@
             pltpu.VMEM((wide, own * frame_count, channels), f32),
             pltpu.VMEM((n, 2, channels), f32),
             pltpu.VMEM((n, 2, channels), f32),
-            dma((15,)),
+            dma((12,)),
             dma((2,)),
-            dma((2,)),
-            dma((3,)),
+            dma,
             dma((3,)),
         ],
         compiler_params=pltpu.CompilerParams(

time: 17.3 us -> 17.2 us (level)
  no operation moved by 1% of the time
where the time goes in v4:
time: 17.2 us; the launch traced here: 16.9 us
  Pallas kernels  16.9 us (98%)
    pallas_call x1, Pallas kernels, one_frame_each(): pl.pallas_call(functools.partial(fused_kernel, n), out_shape=passed, in_s...  15 us
    pallas_call x1, Pallas kernels, one_frame_each(): pl.pallas_call(functools.partial(last_kernel, n), out_shape=jax.ShapeDtyp...  1.97 us

profile of v4, /device:TPU:0, one launch (start us, length us, event | category | flops | bytes accessed | tf_op | source)
XLA Modules:
  0.0 16.9 jit_solution(5944866250453104645)
XLA Ops:
  0.0 15.0 %shard_map.136 = (f32[1280,128]{1,0:T(8,128)S(1)}, f32[1280,128]{1,0:T(8,128)S(1)}, f32[8,128]{1,0:T(8,128)S(1)}, bf16[3,4,384,256]{3,2,1,0:T(8,128)(2,1)S(1)}) custom-call(bf16[3,16,48]{2,1,0:T(8,128)(2,1)} %bitcast.8, s32[16]{0:T(128)} %owner_any.1, s32[8]{0:T(128)} %picks_any.1, bf16[768,1024]{1,0:T(8,128)(2,1)} %patch_any.1, f32[1,1024]{1,0:T(1,128)} %bitcast.9, ...), custom_call_target="tpu_custom_call" | custom-call | tf_op jit(solution)/shard_map/pallas_call | solution.py:799
  15.0 2.0 %shard_map.137 = bf16[3,8,2,16,128]{4,3,2,1,0:T(8,128)(2,1)} custom-call(f32[1280,128]{1,0:T(8,128)S(1)} %get-tuple-element.9.ready, f32[1280,128]{1,0:T(8,128)S(1)} %get-tuple-element.10.normed_ref, f32[8,128]{1,0:T(8,128)S(1)} %get-tuple-element.11.terms, bf16[3,4,384,256]{3,2,1,0:T(8,128)(2,1)S(1)} %get-tuple-element.12.turned), custom_call_target="tpu_custom_call" | custom-call | tf_op jit(solution)/shard_map/pallas_call | solution.py:859

commit v5 on v4

--- a/solution.py
+++ b/solution.py
@@ -248,7 +248,6 @@
     sums_one,
     sums_two,
     local_sem,
-    halo_recv,
     send_sem,
     recv_sem,
 ):
@@ -290,7 +289,7 @@
         pltpu.make_async_copy(
             patch_any.at[pl.ds(part * third, third)],
             patch_w.at[pl.ds(part * third, third)],
-            local_sem.at[7 + part],
+            local_sem.at[2 + part],
         )
         for part in range(3)
     ]
@@ -298,29 +297,27 @@
         pltpu.make_async_copy(
             head_any.at[pl.ds(part * part_rows, part_rows)],
             head_w.at[pl.ds(part * part_rows, part_rows)],
-            local_sem.at[10 + part],
+            local_sem.at[5 + part],
         )
         for part in range(2)
     ]
-    load_inner = pltpu.make_async_copy(inner_any, inner_w, local_sem.at[4])
-    load_out = pltpu.make_async_copy(out_weight_any, out_weight, local_sem.at[5])
-    load_owner = pltpu.make_async_copy(owner_any, owner, local_sem.at[5])
-    load_picks = pltpu.make_async_copy(picks_any, picks, local_sem.at[5])
+    load_inner = pltpu.make_async_copy(inner_any, inner_w, local_sem.at[7])
+    load_out = pltpu.make_async_copy(out_weight_any, out_weight, local_sem.at[7])
+    load_owner = pltpu.make_async_copy(owner_any, owner, local_sem.at[7])
+    load_picks = pltpu.make_async_copy(picks_any, picks, local_sem.at[7])
     load_wide = [
-        pltpu.make_async_copy(source, wide_rows.at[index], local_sem.at[6])
+        pltpu.make_async_copy(source, wide_rows.at[index], local_sem.at[1])
         for index, source in enumerate((patch_bias_any, norm_gain_any, head_bias_any, head_out_any))
     ]
     load_group = [
-        pltpu.make_async_copy(source, group_rows.at[index], local_sem.at[5])
+        pltpu.make_async_copy(source, group_rows.at[index], local_sem.at[7])
         for index, source in enumerate((group_gain_any, group_shift_any))
     ]
     load_frames.start()
     load_hidden.start()
-    for load in load_patch:
-        load.start()
     for load in load_wide:
         load.start()
-    for load in load_head:
+    for load in load_patch + load_head:
         load.start()
     load_owner.start()
     load_picks.start()
@@ -376,6 +373,7 @@
     sent[...] = jnp.zeros_like(sent)
 
     load_hidden.wait()
+    pltpu.make_async_copy(wide_rows, wide_rows, local_sem.at[1]).wait()
     first = jnp.zeros((1, channels), jnp.float32)
     second = jnp.zeros((1, channels), jnp.float32)
     for row in range(own):
@@ -385,7 +383,6 @@
     first, second = group_sums(first, second)
     sums_one[me] = jnp.where(spot == 0, first, second)
 
-    pltpu.make_async_copy(wide_rows, wide_rows, local_sem.at[6]).wait()
     embedded = wide_rows[0]
     for part in range(3):
         load_patch[part].wait()
@@ -424,8 +421,9 @@
     )
     load_owner.wait()
     load_picks.wait()
-    pltpu.make_async_copy(group_rows, group_rows, local_sem.at[5]).wait()
+    pltpu.make_async_copy(group_rows, group_rows, local_sem.at[7]).wait()
     load_out.wait()
+    load_inner.wait()
     mine = owner[me]
     picked = jnp.float32(0.0)
     for pick in range(picks.shape[0]):
@@ -504,7 +502,7 @@
         src_ref=hidden_any.at[pl.ds(own - 1, 1)],
         dst_ref=hidden.at[pl.ds(0, 1)],
         send_sem=send_sem,
-        recv_sem=halo_recv.at[0],
+        recv_sem=recv_sem.at[3],
         device_id={"row": lax.rem(me + 1, n)},
         device_id_type=MESH,
     )
@@ -512,7 +510,7 @@
         src_ref=hidden_any.at[pl.ds(0, 1)],
         dst_ref=hidden.at[pl.ds(own + 1, 1)],
         send_sem=send_sem,
-        recv_sem=halo_recv.at[1],
+        recv_sem=recv_sem.at[4],
         device_id={"row": lax.rem(me + n - 1, n)},
         device_id_type=MESH,
     )
@@ -582,24 +580,23 @@
     for row in range(1, own + 1):
         spread_cells(row)
 
-    load_inner.wait()
     for row_tap in range(3):
         for col_tap in range(3):
             part = pl.ds(col_tap * channels, channels)
             for time_tap in range(3):
                 block = inner_w[time_tap, row_tap, col_tap].T
-                turned[row_tap, 2 - time_tap, part, 0:channels] = block
-                turned[row_tap, 3 - time_tap, part, channels:] = block
+                turned[2 - row_tap, 2 - time_tap, part, 0:channels] = block
+                turned[2 - row_tap, 3 - time_tap, part, channels:] = block
             empty = jnp.zeros((channels, channels), jnp.bfloat16)
-            turned[row_tap, 3, part, 0:channels] = empty
-            turned[row_tap, 0, part, channels:] = empty
+            turned[2 - row_tap, 3, part, 0:channels] = empty
+            turned[2 - row_tap, 0, part, channels:] = empty
     from_peers(sums_one, 0)
+    from_peers(arrived, 1)
     means = over_devices(sums_one) / cell_total
     group_mean = means[0:1]
     inverse = lax.rsqrt(means[1:2] - group_mean * group_mean + eps_norm)
     group_gain = group_rows[0]
     group_shift = group_rows[1]
-    from_peers(arrived, 1)
     def pixel_taps(row, block):
         for row_tap in range(3):
             for time_tap in range(3):
@@ -737,30 +734,32 @@
             windows[row, 0 : FRAMES // 2, :, :, col_tap * channels : (col_tap + 1) * channels] = (
                 shifted.astype(jnp.bfloat16).reshape(FRAMES // 2, 2, wide, channels)
             )
+    half_line = line // 2
+    taken = jnp.concatenate(
+        [
+            windows[
+                above : above + own, ahead // 2 : ahead // 2 + FRAMES // 2, ahead % 2
+            ].reshape(own * half_line, 3 * channels)
+            for above in range(3)
+            for ahead in range(4)
+        ],
+        axis=1,
+    )
+    summed = jnp.dot(
+        taken,
+        turned[...].reshape(12 * 3 * channels, 2 * channels),
+        preferred_element_type=jnp.float32,
+    )
     for row in range(own):
-        taken = jnp.concatenate(
-            [
-                windows[
-                    row + 2 - row_tap, ahead // 2 : ahead // 2 + FRAMES // 2, ahead % 2
-                ].reshape(line // 2, 3 * channels)
-                for row_tap in range(3)
-                for ahead in range(4)
-            ],
-            axis=1,
-        )
-        summed = jnp.dot(
-            taken,
-            turned[...].reshape(12 * 3 * channels, 2 * channels),
-            preferred_element_type=jnp.float32,
-        )
         for side in range(2):
             out[row, :, side] = (
-                summed[:, side * channels : (side + 1) * channels]
+                summed[
+                    row * half_line : (row + 1) * half_line, side * channels : (side + 1) * channels
+                ]
                 .reshape(FRAMES // 2, wide, channels)
                 .astype(jnp.bfloat16)
             )
-        copy = pltpu.make_async_copy(out.at[row], out_any.at[row], out_sem)
-        copy.start()
+        pltpu.make_async_copy(out.at[row], out_any.at[row], out_sem).start()
     pltpu.make_async_copy(out, out_any, out_sem).wait()
 
 
@@ -826,10 +825,9 @@
             pltpu.VMEM((wide, own * frame_count, channels), f32),
             pltpu.VMEM((n, 2, channels), f32),
             pltpu.VMEM((n, 2, channels), f32),
-            dma((12,)),
-            dma((2,)),
+            dma((8,)),
             dma,
-            dma((3,)),
+            dma((5,)),
         ],
         compiler_params=pltpu.CompilerParams(
             collective_id=0, has_side_effects=True, vmem_limit_bytes=32 << 20

time: 17.2 us -> 17 us (0.988)
  Pallas kernels: 16.9 us -> 16.7 us
where the time goes in v5:
time: 17 us; the launch traced here: 16.7 us
  Pallas kernels  16.7 us (98%)
    pallas_call x1, Pallas kernels, one_frame_each(): pl.pallas_call(functools.partial(fused_kernel, n), out_shape=passed, in_s...  14.9 us
    pallas_call x1, Pallas kernels, one_frame_each(): pl.pallas_call(functools.partial(last_kernel, n), out_shape=jax.ShapeDtyp...  1.82 us

profile of v5, /device:TPU:0, one launch (start us, length us, event | category | flops | bytes accessed | tf_op | source)
XLA Modules:
  0.0 16.7 jit_solution(14751562494028489573)
XLA Ops:
  0.0 14.9 %shard_map.136 = (f32[1280,128]{1,0:T(8,128)S(1)}, f32[1280,128]{1,0:T(8,128)S(1)}, f32[8,128]{1,0:T(8,128)S(1)}, bf16[3,4,384,256]{3,2,1,0:T(8,128)(2,1)S(1)}) custom-call(bf16[3,16,48]{2,1,0:T(8,128)(2,1)} %bitcast.8, s32[16]{0:T(128)} %owner_any.1, s32[8]{0:T(128)} %picks_any.1, bf16[768,1024]{1,0:T(8,128)(2,1)} %patch_any.1, f32[1,1024]{1,0:T(1,128)} %bitcast.9, ...), custom_call_target="tpu_custom_call" | custom-call | tf_op jit(solution)/shard_map/pallas_call | solution.py:798
  14.9 1.8 %shard_map.137 = bf16[3,8,2,16,128]{4,3,2,1,0:T(8,128)(2,1)} custom-call(f32[1280,128]{1,0:T(8,128)S(1)} %get-tuple-element.9.ready, f32[1280,128]{1,0:T(8,128)S(1)} %get-tuple-element.10.normed_ref, f32[8,128]{1,0:T(8,128)S(1)} %get-tuple-element.11.terms, bf16[3,4,384,256]{3,2,1,0:T(8,128)(2,1)S(1)} %get-tuple-element.12.turned), custom_call_target="tpu_custom_call" | custom-call | tf_op jit(solution)/shard_map/pallas_call | solution.py:857

commit v6 on v5

--- a/solution.py
+++ b/solution.py
@@ -223,6 +223,7 @@
     normed_ref,
     terms,
     turned,
+    paired,
     frames,
     owner,
     picks,
@@ -580,16 +581,25 @@
     for row in range(1, own + 1):
         spread_cells(row)
 
+    empty = jnp.zeros((channels, channels), jnp.bfloat16)
     for row_tap in range(3):
+        above = 2 - row_tap
         for col_tap in range(3):
             part = pl.ds(col_tap * channels, channels)
-            for time_tap in range(3):
-                block = inner_w[time_tap, row_tap, col_tap].T
-                turned[2 - row_tap, 2 - time_tap, part, 0:channels] = block
-                turned[2 - row_tap, 3 - time_tap, part, channels:] = block
-            empty = jnp.zeros((channels, channels), jnp.bfloat16)
-            turned[2 - row_tap, 3, part, 0:channels] = empty
-            turned[2 - row_tap, 0, part, channels:] = empty
+            blocks = [inner_w[time_tap, row_tap, col_tap].T for time_tap in range(3)]
+            for ahead in range(2):
+                turned[above, ahead, part, 0:channels] = blocks[1 - ahead]
+                turned[above, ahead, part, channels:] = blocks[2 - ahead]
+            for side in range(2):
+                at = (2 - col_tap + side) * channels
+                for kind in range(2):
+                    paired[kind, above, at : at + channels, side * channels : (side + 1) * channels] = (
+                        blocks[2 - 2 * kind]
+                    )
+        for kind in range(2):
+            paired[kind, above, 3 * channels :, 0:channels] = empty
+            paired[kind, above, 0:channels, channels:] = empty
+
     from_peers(sums_one, 0)
     from_peers(arrived, 1)
     means = over_devices(sums_one) / cell_total
@@ -713,49 +723,86 @@
     terms[0:2] = total * (inverse / cell_total)
 
 
-def last_kernel(n, ready, normed_ref, terms, turned, out_any, windows, out, out_sem):
+def last_kernel(
+    n, ready, normed_ref, terms, turned, paired, out_any, padded, windows, pairs, rest, out, out_sem
+):
     me = lax.axis_index("row")
     own = out.shape[0]
     wide = out.shape[3]
     channels = out.shape[4]
     line = FRAMES * wide
     windows[:, FRAMES // 2] = jnp.zeros((own + 2, 2, wide, 3 * channels), jnp.bfloat16)
-    position = lax.rem(lax.broadcasted_iota(jnp.int32, (line, channels), 0), wide)
+    pairs[1, :, FRAMES // 2 - 1] = jnp.zeros((own + 2, wide // 2, 4 * channels), jnp.bfloat16)
+    pitch = wide + 1
+    blank = jnp.zeros((1, channels), jnp.float32)
+    for cell in range((own + 2) * FRAMES + 1):
+        padded[cell * pitch : cell * pitch + 1] = blank
+    first_part = jnp.broadcast_to(terms[0:1], (wide, channels))
+    second_part = jnp.broadcast_to(terms[1:2], (wide, channels))
     for row in range(own + 2):
-        part = pl.ds(row * line, line)
-        state_grad = ready[part] - terms[0:1] - normed_ref[part] * terms[1:2]
-        if row == 0:
-            state_grad = jnp.where(me > 0, state_grad, 0.0)
-        if row == own + 1:
-            state_grad = jnp.where(me < n - 1, state_grad, 0.0)
-        after = jnp.where(position == wide - 1, 0.0, pltpu.roll(state_grad, line - 1, 0))
-        earlier = jnp.where(position == 0, 0.0, pltpu.roll(state_grad, 1, 0))
-        for col_tap, shifted in enumerate((after, state_grad, earlier)):
-            windows[row, 0 : FRAMES // 2, :, :, col_tap * channels : (col_tap + 1) * channels] = (
-                shifted.astype(jnp.bfloat16).reshape(FRAMES // 2, 2, wide, channels)
-            )
+        for frame in range(FRAMES):
+            cell = row * FRAMES + frame
+            part = pl.ds(cell * wide, wide)
+            state_grad = ready[part] - first_part - normed_ref[part] * second_part
+            if row == 0:
+                state_grad = jnp.where(me > 0, state_grad, 0.0)
+            if row == own + 1:
+                state_grad = jnp.where(me < n - 1, state_grad, 0.0)
+            at = cell * pitch + 1
+            padded[at : at + wide] = state_grad
+            for col_tap in range(3):
+                windows[
+                    row, frame // 2, frame % 2, :, col_tap * channels : (col_tap + 1) * channels
+                ] = padded[at + 1 - col_tap : at + 1 - col_tap + wide].astype(jnp.bfloat16)
+            kind, step = frame % 2, frame // 2 - frame % 2
+            if step >= 0:
+                for index in range(4):
+                    pairs[kind, row, step, :, index * channels : (index + 1) * channels] = padded[
+                        pl.ds(cell * pitch + index, wide // 2, stride=2)
+                    ].astype(jnp.bfloat16)
     half_line = line // 2
+    for kind in range(2):
+        left = jnp.concatenate(
+            [
+                pairs[kind, above : above + own].reshape(own * half_line // 2, 4 * channels)
+                for above in range(3)
+            ],
+            axis=1,
+        )
+        both = jnp.dot(
+            left,
+            paired[kind].reshape(12 * channels, 2 * channels),
+            preferred_element_type=jnp.float32,
+        )
+        for side in range(2):
+            rest[kind, pl.ds(side, own * half_line // 2, stride=2)] = both[
+                :, side * channels : (side + 1) * channels
+            ]
     taken = jnp.concatenate(
         [
             windows[
                 above : above + own, ahead // 2 : ahead // 2 + FRAMES // 2, ahead % 2
             ].reshape(own * half_line, 3 * channels)
             for above in range(3)
-            for ahead in range(4)
+            for ahead in (1, 2)
         ],
         axis=1,
     )
     summed = jnp.dot(
         taken,
-        turned[...].reshape(12 * 3 * channels, 2 * channels),
+        turned[...].reshape(6 * 3 * channels, 2 * channels),
         preferred_element_type=jnp.float32,
     )
     for row in range(own):
         for side in range(2):
             out[row, :, side] = (
-                summed[
-                    row * half_line : (row + 1) * half_line, side * channels : (side + 1) * channels
-                ]
+                (
+                    summed[
+                        row * half_line : (row + 1) * half_line,
+                        side * channels : (side + 1) * channels,
+                    ]
+                    + rest[side, row * half_line : (row + 1) * half_line]
+                )
                 .reshape(FRAMES // 2, wide, channels)
                 .astype(jnp.bfloat16)
             )
@@ -793,13 +840,14 @@
         pltpu.VMEM((cells, channels), f32),
         pltpu.VMEM((cells, channels), f32),
         pltpu.VMEM((8, channels), f32),
-        pltpu.VMEM((3, 4, 3 * channels, 2 * channels), bf16),
+        pltpu.VMEM((3, 2, 3 * channels, 2 * channels), bf16),
+        pltpu.VMEM((2, 3, 4 * channels, 2 * channels), bf16),
     ]
     kept = pl.pallas_call(
         functools.partial(fused_kernel, n),
         out_shape=passed,
         in_specs=[pl.BlockSpec(memory_space=pltpu.HBM)] * 14,
-        out_specs=[vmem] * 4,
+        out_specs=[vmem] * 5,
         scratch_shapes=[
             pltpu.VMEM((3, strip, height), bf16),
             pltpu.SMEM(frame_owner.shape, jnp.int32),
@@ -857,10 +905,13 @@
     return pl.pallas_call(
         functools.partial(last_kernel, n),
         out_shape=jax.ShapeDtypeStruct(out_shape, bf16),
-        in_specs=[vmem] * 4,
+        in_specs=[vmem] * 5,
         out_specs=pl.BlockSpec(memory_space=pltpu.HBM),
         scratch_shapes=[
+            pltpu.VMEM((-(-((own + 2) * frame_count * (wide + 1) + 1) // 8) * 8, channels), f32),
             pltpu.VMEM((own + 2, frame_count // 2 + 1, 2, wide, 3 * channels), bf16),
+            pltpu.VMEM((2, own + 2, frame_count // 2, wide // 2, 4 * channels), bf16),
+            pltpu.VMEM((2, own * frame_count * wide // 2, channels), f32),
             pltpu.VMEM(out_shape, bf16),
             dma,
         ],

time: 17 us -> 16.8 us (0.988)
  no operation moved by 1% of the time
where the time goes in v6:
time: 16.8 us; the launch traced here: 16.6 us
  Pallas kernels  16.6 us (99%)
    pallas_call x1, Pallas kernels, one_frame_each(): pl.pallas_call(functools.partial(fused_kernel, n), out_shape=passed, in_s...  14.9 us
    pallas_call x1, Pallas kernels, one_frame_each(): pl.pallas_call(functools.partial(last_kernel, n), out_shape=jax.ShapeDtyp...  1.68 us

profile of v6, /device:TPU:0, one launch (start us, length us, event | category | flops | bytes accessed | tf_op | source)
XLA Modules:
  0.0 16.6 jit_solution(11096011694120797395)
XLA Ops:
  0.0 14.9 %shard_map.136 = (f32[1280,128]{1,0:T(8,128)S(1)}, f32[1280,128]{1,0:T(8,128)S(1)}, f32[8,128]{1,0:T(8,128)S(1)}, bf16[3,2,384,256]{3,2,1,0:T(8,128)(2,1)S(1)}, bf16[2,3,512,256]{3,2,1,0:T(8,128)(2,1)S(1)}) custom-call(bf16[3,16,48]{2,1,0:T(8,128)(2,1)} %bitcast.8, s32[16]{0:T(128)} %owner_any.1, s32[8]{0:T(128)} %picks_any.1, bf16[768,1024]{1,0:T(8,128)(2,1)} %patch_any.1, ...), custom_call_target="tpu_custom_call" | custom-call | tf_op jit(solution)/shard_map/pallas_call | solution.py:846
  14.9 1.7 %shard_map.137 = bf16[3,8,2,16,128]{4,3,2,1,0:T(8,128)(2,1)} custom-call(f32[1280,128]{1,0:T(8,128)S(1)} %get-tuple-element.10.ready, f32[1280,128]{1,0:T(8,128)S(1)} %get-tuple-element.11.normed_ref, f32[8,128]{1,0:T(8,128)S(1)} %get-tuple-element.12.terms, bf16[3,2,384,256]{3,2,1,0:T(8,128)(2,1)S(1)} %get-tuple-element.13.turned, ...), custom_call_target="tpu_custom_call" | custom-call | tf_op jit(solution)/shard_map/pallas_call | solution.py:905

commit v7 on v6

--- a/solution.py
+++ b/solution.py
@@ -691,6 +691,7 @@
                 )
                 at = (2 * side + index) * FRAMES
                 slope[part] = several[at : at + FRAMES] * state_terms(part)[1]
+    terms[2:3] = inverse / cell_total
     for cell in range((own + 2) * FRAMES):
         part = pl.ds(cell * wide, wide)
         ready[part] = slope[cell * pitch : cell * pitch + wide] * spread
@@ -710,17 +711,7 @@
         to_left.wait_send()
 
     from_peers(sums_two, 2)
-    total = over_devices(sums_two)
-    lane = lax.broadcasted_iota(jnp.int32, total.shape, 1)
-    step = 1
-    while step < per_group:
-        total = total + jnp.where(
-            lax.rem(lane // step, 2) == 0,
-            pltpu.roll(total, channels - step, 1),
-            pltpu.roll(total, step, 1),
-        )
-        step *= 2
-    terms[0:2] = total * (inverse / cell_total)
+    terms[0:2] = over_devices(sums_two)
 
 
 def last_kernel(
@@ -731,14 +722,25 @@
     wide = out.shape[3]
     channels = out.shape[4]
     line = FRAMES * wide
-    windows[:, FRAMES // 2] = jnp.zeros((own + 2, 2, wide, 3 * channels), jnp.bfloat16)
+    windows[:, FRAMES // 2, 0] = jnp.zeros((own + 2, wide, 3 * channels), jnp.bfloat16)
     pairs[1, :, FRAMES // 2 - 1] = jnp.zeros((own + 2, wide // 2, 4 * channels), jnp.bfloat16)
     pitch = wide + 1
     blank = jnp.zeros((1, channels), jnp.float32)
     for cell in range((own + 2) * FRAMES + 1):
         padded[cell * pitch : cell * pitch + 1] = blank
-    first_part = jnp.broadcast_to(terms[0:1], (wide, channels))
-    second_part = jnp.broadcast_to(terms[1:2], (wide, channels))
+    total = terms[0:2]
+    lane = lax.broadcasted_iota(jnp.int32, total.shape, 1)
+    step = 1
+    while step < channels // GROUPS:
+        total = total + jnp.where(
+            lax.rem(lane // step, 2) == 0,
+            pltpu.roll(total, channels - step, 1),
+            pltpu.roll(total, step, 1),
+        )
+        step *= 2
+    total = total * terms[2:3]
+    first_part = jnp.broadcast_to(total[0:1], (wide, channels))
+    second_part = jnp.broadcast_to(total[1:2], (wide, channels))
     for row in range(own + 2):
         for frame in range(FRAMES):
             cell = row * FRAMES + frame
@@ -750,7 +752,7 @@
                 state_grad = jnp.where(me < n - 1, state_grad, 0.0)
             at = cell * pitch + 1
             padded[at : at + wide] = state_grad
-            for col_tap in range(3):
+            for col_tap in range(3 if frame > 0 else 0):
                 windows[
                     row, frame // 2, frame % 2, :, col_tap * channels : (col_tap + 1) * channels
                 ] = padded[at + 1 - col_tap : at + 1 - col_tap + wide].astype(jnp.bfloat16)

time: 16.8 us -> 16.8 us (level)
  no operation moved by 1% of the time
where the time goes in v7:
time: 16.8 us; the launch traced here: 16.6 us
  Pallas kernels  16.6 us (99%)
    pallas_call x1, Pallas kernels, one_frame_each(): pl.pallas_call(functools.partial(fused_kernel, n), out_shape=passed, in_s...  14.8 us
    pallas_call x1, Pallas kernels, one_frame_each(): pl.pallas_call(functools.partial(last_kernel, n), out_shape=jax.ShapeDtyp...  1.82 us

profile of v7, /device:TPU:0, one launch (start us, length us, event | category | flops | bytes accessed | tf_op | source)
XLA Modules:
  0.0 16.6 jit_solution(10232242065212974368)
XLA Ops:
  0.0 14.8 %shard_map.136 = (f32[1280,128]{1,0:T(8,128)S(1)}, f32[1280,128]{1,0:T(8,128)S(1)}, f32[8,128]{1,0:T(8,128)S(1)}, bf16[3,2,384,256]{3,2,1,0:T(8,128)(2,1)S(1)}, bf16[2,3,512,256]{3,2,1,0:T(8,128)(2,1)S(1)}) custom-call(bf16[3,16,48]{2,1,0:T(8,128)(2,1)} %bitcast.8, s32[16]{0:T(128)} %owner_any.1, s32[8]{0:T(128)} %picks_any.1, bf16[768,1024]{1,0:T(8,128)(2,1)} %patch_any.1, ...), custom_call_target="tpu_custom_call" | custom-call | tf_op jit(solution)/shard_map/pallas_call | solution.py:848
  14.8 1.8 %shard_map.137 = bf16[3,8,2,16,128]{4,3,2,1,0:T(8,128)(2,1)} custom-call(f32[1280,128]{1,0:T(8,128)S(1)} %get-tuple-element.10.ready, f32[1280,128]{1,0:T(8,128)S(1)} %get-tuple-element.11.normed_ref, f32[8,128]{1,0:T(8,128)S(1)} %get-tuple-element.12.terms, bf16[3,2,384,256]{3,2,1,0:T(8,128)(2,1)S(1)} %get-tuple-element.13.turned, ...), custom_call_target="tpu_custom_call" | custom-call | tf_op jit(solution)/shard_map/pallas_call | solution.py:907

commit v8 on v7

--- a/solution.py
+++ b/solution.py
@@ -244,8 +244,6 @@
     band,
     slope,
     cells,
-    factor,
-    centred_cells,
     sums_one,
     sums_two,
     local_sem,
@@ -286,32 +284,33 @@
     load_hidden = pltpu.make_async_copy(hidden_any, hidden.at[pl.ds(1, own)], local_sem.at[1])
     pix, width = patch_w.shape
     third, part_rows = pix // 3, width // 2
+    pieces = ((0, 2 * third), (2 * third, pix))
     load_patch = [
         pltpu.make_async_copy(
-            patch_any.at[pl.ds(part * third, third)],
-            patch_w.at[pl.ds(part * third, third)],
+            patch_any.at[pl.ds(low, high - low)],
+            patch_w.at[pl.ds(low, high - low)],
             local_sem.at[2 + part],
         )
-        for part in range(3)
+        for part, (low, high) in enumerate(pieces)
     ]
     load_head = [
         pltpu.make_async_copy(
             head_any.at[pl.ds(part * part_rows, part_rows)],
             head_w.at[pl.ds(part * part_rows, part_rows)],
-            local_sem.at[5 + part],
+            local_sem.at[4 + part],
         )
         for part in range(2)
     ]
-    load_inner = pltpu.make_async_copy(inner_any, inner_w, local_sem.at[7])
-    load_out = pltpu.make_async_copy(out_weight_any, out_weight, local_sem.at[7])
-    load_owner = pltpu.make_async_copy(owner_any, owner, local_sem.at[7])
-    load_picks = pltpu.make_async_copy(picks_any, picks, local_sem.at[7])
+    load_inner = pltpu.make_async_copy(inner_any, inner_w, local_sem.at[6])
+    load_out = pltpu.make_async_copy(out_weight_any, out_weight, local_sem.at[6])
+    load_owner = pltpu.make_async_copy(owner_any, owner, local_sem.at[6])
+    load_picks = pltpu.make_async_copy(picks_any, picks, local_sem.at[6])
     load_wide = [
         pltpu.make_async_copy(source, wide_rows.at[index], local_sem.at[1])
         for index, source in enumerate((patch_bias_any, norm_gain_any, head_bias_any, head_out_any))
     ]
     load_group = [
-        pltpu.make_async_copy(source, group_rows.at[index], local_sem.at[7])
+        pltpu.make_async_copy(source, group_rows.at[index], local_sem.at[6])
         for index, source in enumerate((group_gain_any, group_shift_any))
     ]
     load_frames.start()
@@ -385,11 +384,11 @@
     sums_one[me] = jnp.where(spot == 0, first, second)
 
     embedded = wide_rows[0]
-    for part in range(3):
+    for part, (low, high) in enumerate(pieces):
         load_patch[part].wait()
         embedded = embedded + jnp.dot(
-            tokens[:, part * third : (part + 1) * third].astype(jnp.bfloat16),
-            patch_w[part * third : (part + 1) * third],
+            tokens[:, low:high].astype(jnp.bfloat16),
+            patch_w[low:high],
             preferred_element_type=jnp.float32,
         )
     centred = embedded - jnp.mean(embedded, axis=1, keepdims=True)
@@ -422,7 +421,7 @@
     )
     load_owner.wait()
     load_picks.wait()
-    pltpu.make_async_copy(group_rows, group_rows, local_sem.at[7]).wait()
+    pltpu.make_async_copy(group_rows, group_rows, local_sem.at[6]).wait()
     load_out.wait()
     load_inner.wait()
     mine = owner[me]
@@ -625,16 +624,14 @@
         return centred, silu_slope(centred * spread + group_shift)
 
     own_cells = own * FRAMES
-    for w in range(wide):
-        part = pl.ds(FRAMES * pitch + w, own_cells, stride=pitch)
-        centred_cells[w], factor[w] = state_terms(part)
     for frame in range(FRAMES):
         for row in range(half):
             by_frame[row, frame : frame + 1, :] = arrived[slot_of[frame], row]
     for row in range(1, own + 1):
         pixel_taps(row, ((row - 1) * FRAMES, own_cells + (row - 1) * FRAMES))
     left = columns[0 : 2 * own_cells].astype(jnp.bfloat16)
-    firsts, seconds = [], []
+    first = jnp.zeros((8, channels), jnp.float32)
+    second = jnp.zeros((8, channels), jnp.float32)
     for output in range(0, window, 2):
         lanes = pl.ds(output * channels, min(2, window - output) * channels)
         several = jnp.dot(left, band[:, lanes], preferred_element_type=jnp.float32)
@@ -643,20 +640,20 @@
                 w = output + index + side * (wide - window)
                 if side == 0 and output + index == window - 1 or side == 1 and output + index == 0:
                     continue
+                centred, slope_factor = state_terms(
+                    pl.ds(FRAMES * pitch + w, own_cells, stride=pitch)
+                )
                 upstream = (
                     several[
                         side * own_cells : (side + 1) * own_cells,
                         index * channels : (index + 1) * channels,
                     ]
-                    * factor[w]
+                    * slope_factor
                 )
-                slope[pl.ds(FRAMES * pitch + w, own_cells, stride=pitch)] = upstream
-                firsts.append(jnp.sum(upstream.reshape(-1, 8, channels), axis=0))
-                seconds.append(
-                    jnp.sum((upstream * centred_cells[w]).reshape(-1, 8, channels), axis=0)
+                first = first + jnp.sum(upstream.reshape(-1, 8, channels), axis=0)
+                second = second + jnp.sum(
+                    (upstream * centred).reshape(-1, 8, channels), axis=0
                 )
-    first = tree_sum(firsts)
-    second = tree_sum(seconds)
     first = jnp.sum(first, axis=0, keepdims=True) * group_gain
     second = jnp.sum(second, axis=0, keepdims=True) * spread
     sums_two[me] = jnp.where(spot == 0, first, second)
@@ -675,7 +672,7 @@
     for index, row in enumerate((0, own + 1)):
         pixel_taps(row, (2 * own_cells + index * FRAMES, 2 * own_cells + (2 + index) * FRAMES))
         spread_cells(row)
-    left = columns[2 * own_cells :].astype(jnp.bfloat16)
+    left = columns[...].astype(jnp.bfloat16)
     for output in range(window):
         several = jnp.dot(
             left,
@@ -685,11 +682,14 @@
         for side in range(2):
             if side == 0 and output == window - 1 or side == 1 and output == 0:
                 continue
+            w = output + side * (wide - window)
+            part = pl.ds(FRAMES * pitch + w, own_cells, stride=pitch)
+            slope[part] = (
+                several[side * own_cells : (side + 1) * own_cells] * state_terms(part)[1]
+            )
             for index, row in enumerate((0, own + 1)):
-                part = pl.ds(
-                    row * FRAMES * pitch + output + side * (wide - window), FRAMES, stride=pitch
-                )
-                at = (2 * side + index) * FRAMES
+                part = pl.ds(row * FRAMES * pitch + w, FRAMES, stride=pitch)
+                at = 2 * own_cells + (2 * side + index) * FRAMES
                 slope[part] = several[at : at + FRAMES] * state_terms(part)[1]
     terms[2:3] = inverse / cell_total
     for cell in range((own + 2) * FRAMES):
@@ -871,11 +871,9 @@
             pltpu.VMEM((depth, window * channels), bf16),
             pltpu.VMEM(((own + 2) * frame_count * (wide + 1), channels), f32),
             pltpu.VMEM(((own + 2) * frame_count * (wide + 1), channels), f32),
-            pltpu.VMEM((wide, own * frame_count, channels), f32),
-            pltpu.VMEM((wide, own * frame_count, channels), f32),
             pltpu.VMEM((n, 2, channels), f32),
             pltpu.VMEM((n, 2, channels), f32),
-            dma((8,)),
+            dma((7,)),
             dma,
             dma((5,)),
         ],

time: 16.8 us -> 16.8 us (level)
  no operation moved by 1% of the time
where the time goes in v8:
time: 16.8 us; the launch traced here: 16.6 us
  Pallas kernels  16.6 us (99%)
    pallas_call x1, Pallas kernels, one_frame_each(): pl.pallas_call(functools.partial(fused_kernel, n), out_shape=passed, in_s...  14.8 us
    pallas_call x1, Pallas kernels, one_frame_each(): pl.pallas_call(functools.partial(last_kernel, n), out_shape=jax.ShapeDtyp...  1.82 us

profile of v8, /device:TPU:0, one launch (start us, length us, event | category | flops | bytes accessed | tf_op | source)
XLA Modules:
  0.0 16.6 jit_solution(14143713034930778475)
XLA Ops:
  0.0 14.8 %shard_map.136 = (f32[1280,128]{1,0:T(8,128)S(1)}, f32[1280,128]{1,0:T(8,128)S(1)}, f32[8,128]{1,0:T(8,128)S(1)}, bf16[3,2,384,256]{3,2,1,0:T(8,128)(2,1)S(1)}, bf16[2,3,512,256]{3,2,1,0:T(8,128)(2,1)S(1)}) custom-call(bf16[3,16,48]{2,1,0:T(8,128)(2,1)} %bitcast.8, s32[16]{0:T(128)} %owner_any.1, s32[8]{0:T(128)} %picks_any.1, bf16[768,1024]{1,0:T(8,128)(2,1)} %patch_any.1, ...), custom_call_target="tpu_custom_call" | custom-call | tf_op jit(solution)/shard_map/pallas_call | solution.py:848
  14.8 1.8 %shard_map.137 = bf16[3,8,2,16,128]{4,3,2,1,0:T(8,128)(2,1)} custom-call(f32[1280,128]{1,0:T(8,128)S(1)} %get-tuple-element.10.ready, f32[1280,128]{1,0:T(8,128)S(1)} %get-tuple-element.11.normed_ref, f32[8,128]{1,0:T(8,128)S(1)} %get-tuple-element.12.terms, bf16[3,2,384,256]{3,2,1,0:T(8,128)(2,1)S(1)} %get-tuple-element.13.turned, ...), custom_call_target="tpu_custom_call" | custom-call | tf_op jit(solution)/shard_map/pallas_call | solution.py:905

commit v9 on v8

--- a/solution.py
+++ b/solution.py
@@ -763,23 +763,6 @@
                         pl.ds(cell * pitch + index, wide // 2, stride=2)
                     ].astype(jnp.bfloat16)
     half_line = line // 2
-    for kind in range(2):
-        left = jnp.concatenate(
-            [
-                pairs[kind, above : above + own].reshape(own * half_line // 2, 4 * channels)
-                for above in range(3)
-            ],
-            axis=1,
-        )
-        both = jnp.dot(
-            left,
-            paired[kind].reshape(12 * channels, 2 * channels),
-            preferred_element_type=jnp.float32,
-        )
-        for side in range(2):
-            rest[kind, pl.ds(side, own * half_line // 2, stride=2)] = both[
-                :, side * channels : (side + 1) * channels
-            ]
     taken = jnp.concatenate(
         [
             windows[
@@ -795,6 +778,23 @@
         turned[...].reshape(6 * 3 * channels, 2 * channels),
         preferred_element_type=jnp.float32,
     )
+    for kind in range(2):
+        left = jnp.concatenate(
+            [
+                pairs[kind, above : above + own].reshape(own * half_line // 2, 4 * channels)
+                for above in range(3)
+            ],
+            axis=1,
+        )
+        both = jnp.dot(
+            left,
+            paired[kind].reshape(12 * channels, 2 * channels),
+            preferred_element_type=jnp.float32,
+        )
+        for side in range(2):
+            rest[kind, pl.ds(side, own * half_line // 2, stride=2)] = both[
+                :, side * channels : (side + 1) * channels
+            ]
     for row in range(own):
         for side in range(2):
             out[row, :, side] = (

time: 16.8 us -> 16.8 us (level)
  no operation moved by 1% of the time
where the time goes in v9:
time: 16.8 us; the launch traced here: 16.6 us
  Pallas kernels  16.6 us (99%)
    pallas_call x1, Pallas kernels, one_frame_each(): pl.pallas_call(functools.partial(fused_kernel, n), out_shape=passed, in_s...  14.8 us
    pallas_call x1, Pallas kernels, one_frame_each(): pl.pallas_call(functools.partial(last_kernel, n), out_shape=jax.ShapeDtyp...  1.83 us

profile of v9, /device:TPU:0, one launch (start us, length us, event | category | flops | bytes accessed | tf_op | source)
XLA Modules:
  0.0 16.6 jit_solution(4395381694670262382)
XLA Ops:
  0.0 14.8 %shard_map.136 = (f32[1280,128]{1,0:T(8,128)S(1)}, f32[1280,128]{1,0:T(8,128)S(1)}, f32[8,128]{1,0:T(8,128)S(1)}, bf16[3,2,384,256]{3,2,1,0:T(8,128)(2,1)S(1)}, bf16[2,3,512,256]{3,2,1,0:T(8,128)(2,1)S(1)}) custom-call(bf16[3,16,48]{2,1,0:T(8,128)(2,1)} %bitcast.8, s32[16]{0:T(128)} %owner_any.1, s32[8]{0:T(128)} %picks_any.1, bf16[768,1024]{1,0:T(8,128)(2,1)} %patch_any.1, ...), custom_call_target="tpu_custom_call" | custom-call | tf_op jit(solution)/shard_map/pallas_call | solution.py:848
  14.8 1.8 %shard_map.137 = bf16[3,8,2,16,128]{4,3,2,1,0:T(8,128)(2,1)} custom-call(f32[1280,128]{1,0:T(8,128)S(1)} %get-tuple-element.10.ready, f32[1280,128]{1,0:T(8,128)S(1)} %get-tuple-element.11.normed_ref, f32[8,128]{1,0:T(8,128)S(1)} %get-tuple-element.12.terms, bf16[3,2,384,256]{3,2,1,0:T(8,128)(2,1)S(1)} %get-tuple-element.13.turned, ...), custom_call_target="tpu_custom_call" | custom-call | tf_op jit(solution)/shard_map/pallas_call | solution.py:905
